TPU v7x, 512 devices: a whole 4x4x16 slice. The times are simulated.
512 devices in a mesh: img: 16 (over x, z_hi), band: 32 (over y, z_lo, core).
Axes of the slice: x: 4, y: 4, z: 16 (z_hi: 4, z_lo: 4; z = z_hi * 4 + z_lo), core: 2. Of those that a mesh axis runs over, the one named last changes fastest.
Arguments:
- latents: bfloat16 [16, 64, 64, 1120], P('img', 'band'), may hold values from -6 to 6
- tangents: bfloat16 [16, 64, 64, 1120], P('img', 'band'), may hold values from -6 to 6
- w_expand: bfloat16 [1120, 5632], P('img', 'band'), may hold values from -0.1875 to 0.1875
- b_expand: bfloat16 [5632], P('band'), may hold values from -3 to 3
- w_depth: bfloat16 [9, 5632], P(None, 'band'), may hold values from -2 to 2
- b_depth: bfloat16 [5632], P('band'), may hold values from -3 to 3
Outputs:
- gated: bfloat16 [16, 64, 64, 2816], P('img', 'band')
- gated_tangent: bfloat16 [16, 64, 64, 2816], P('img', 'band')
All inputs are finite; a program needn't handle non-finite values.
Results may differ from a plain program's by a relative error of at most 0.0057.
Values may be sent and summed in bfloat16 or wider, within the bound.
No kernel may reach another device: no remote copies, remote signals or barrier semaphores. Data moves between devices by JAX's collectives and lax.ppermute only.
A program may use at most 64 MiB of HBM per device.

v0:
```python
import jax
import jax.numpy as jnp
from jax import lax
from jax.sharding import PartitionSpec as P


def extended(cells, sides, width):
    for axis, dim in sides:
        count = lax.axis_size(axis)
        ends = count - 1
        head = lax.slice_in_dim(cells, 0, width, axis=dim)
        tail = lax.slice_in_dim(cells, cells.shape[dim] - width, cells.shape[dim], axis=dim)
        cells = jnp.concatenate(
            [
                lax.ppermute(tail, axis, [(i, (i + 1) % count) for i in range(ends)]),
                cells,
                lax.ppermute(head, axis, [((i + 1) % count, i) for i in range(ends)]),
            ],
            axis=dim,
        )
    return cells


def tangent_act(primal_pre, tangent_pre):
    sigmoid_v = jax.nn.sigmoid(primal_pre)
    value = primal_pre * sigmoid_v
    slope = sigmoid_v * (1.0 + primal_pre * (1.0 - sigmoid_v))
    return (value, slope * tangent_pre)


def depthwise(padded, depth_taps, row_count, col_count):
    total = jnp.zeros(padded.shape[:-3] + (row_count, col_count, padded.shape[-1]), jnp.float32)
    for row_off in range(3):
        for col_off in range(3):
            window = padded[
                ..., row_off : row_off + row_count, col_off : col_off + col_count, :
            ].astype(jnp.float32)
            total = total + window * depth_taps[3 * row_off + col_off].astype(jnp.float32)
    return total


def finish(mixed, depth_bias, half):
    primal_mix = mixed[0] + depth_bias.astype(jnp.float32)
    tangent_mix = mixed[1]
    gate_value, gate_tangent = tangent_act(primal_mix[..., half:], tangent_mix[..., half:])
    gated = primal_mix[..., :half] * gate_value
    gated_tangent = tangent_mix[..., :half] * gate_value + primal_mix[..., :half] * gate_tangent
    return (gated.astype(jnp.bfloat16), gated_tangent.astype(jnp.bfloat16))


def activate(pre_act, expand_bias, token_count):
    bias_cols = expand_bias.astype(jnp.float32)
    value, slope_tangent = tangent_act(pre_act[:token_count] + bias_cols, pre_act[token_count:])
    return jnp.concatenate([value.astype(jnp.bfloat16), slope_tangent.astype(jnp.bfloat16)], 0)


def on_device(latents, tangents, w_expand, b_expand, w_depth, b_depth):
    image_count, row_count, col_count, channels = latents.shape
    depth_taps, expand_bias, depth_bias = (
        lax.all_gather(w_depth, "band", axis=1, tiled=True),
        lax.all_gather(b_expand, "band", axis=0, tiled=True),
        lax.all_gather(b_depth, "band", axis=0, tiled=True),
    )
    full_width = expand_bias.shape[0]
    half = full_width // 2
    both_inputs = jnp.stack([latents, tangents])
    span_rows = both_inputs.shape[2]
    token_count = image_count * span_rows * col_count
    stacked = both_inputs.reshape(2 * token_count, channels)
    weight_rows = lax.all_gather(w_expand, "img", axis=0, tiled=True)
    pre_act = jnp.dot(
        stacked,
        lax.all_gather(weight_rows, "band", axis=1, tiled=True),
        preferred_element_type=jnp.float32,
    )
    activated = activate(pre_act, expand_bias, token_count)
    activated = activated.reshape(2, image_count, span_rows, col_count, full_width)
    padded = extended(activated, (("band", 2),), 1)
    padded = jnp.pad(padded, ((0, 0), (0, 0), (0, 0), (1, 1), (0, 0)))
    mixed = depthwise(padded, depth_taps, row_count, col_count)
    return finish(mixed, depth_bias, half)


def solution(mesh):
    placed = (
        P("img", "band", None, None),
        P("img", "band", None, None),
        P("img", "band"),
        P("band"),
        P(None, "band"),
        P("band"),
    )
    return jax.shard_map(
        on_device,
        mesh=mesh,
        in_specs=placed,
        out_specs=(P("img", "band", None, None), P("img", "band", None, None)),
        check_vma=False,
    )
```

profile of v0, /device:TPU:1, one launch (start us, length us, event | category | flops | bytes accessed | tf_op | source)
XLA Modules:
  0.0 304.1 jit_solution(5817018077975962852)
XLA Ops:
  7.2 0.0 copy-start.3
  7.2 0.0 all-gather.4.cloned.1.call-start
  7.3 59.5 %all-gather = bf16[16,70,176]{2,1,0:T(8,128)(2,1)S(1)} all-gather(bf16[1,70,176]{2,1,0:T(8,128)(2,1)} %bitcast.34), channel_id=1, replica_groups=mesh['img'=16,'band'=32] {'img'}, dimensions={0}, use_global_device_ids=true | all-gather | bytes 418880 | tf_op jit(solution)/shard_map/all_gather | solution.py:70
  66.7 0.2 reshape.144
  67.0 1.0 copy.30
  67.9 0.0 all-gather.4.cloned.1.call-update
  68.0 1.3 dynamic-slice
  69.9 0.2 dynamic-update-slice
  70.2 0.0 copy-done.4
  70.2 0.2 dynamic-update-slice.1
  70.4 139.7 %all-reduce.3 = (bf16[5632]{0:T(1024)(128)(2,1)S(1)}, bf16[5632]{0:T(1024)(128)(2,1)S(1)}) all-reduce(bf16[5632]{0:T(1024)(128)(2,1)S(1)} %dynamic-update-slice, bf16[5632]{0:T(1024)(128)(2,1)S(1)} %dynamic-update-slice.1), channel_id=1, replica_groups=mesh['img'=16,'band'=32] {'band'}, use_global_device_ids=true, to_apply=%add.1 | all-reduce | flops 11264 | bytes 45056
  210.1 0.0 copy-done.1
  210.1 0.1 pad_maximum_fusion.3
  210.2 0.0 all-gather.4.cloned.1.call-done
  210.2 7.0 %fusion.22 = f32[256,5632]{1,0:T(8,128)S(1)} fusion(bf16[256,1120]{1,0:T(8,128)(2,1)S(1)} %bitcast.31, bf16[1120,5632]{0,1:T(8,128)(2,1)} %all-gather.4.cloned.1.call-done), kind=kOutput, calls=%fused_computation.48 | convolution fusion | flops 3229614080 | bytes 18956288 | tf_op jit(solution)/shard_map/dot_general | solution.py:71
  217.2 1.4 multiply_convert_fusion
  218.6 0.2 pad_maximum_fusion.2
  218.8 0.0 copy-start.2
  218.8 1.8 fusion.21
  220.6 8.2 %collective-permute-start.1 = (bf16[2,1,1,64,5632]{4,3,2,1,0:T(8,128)(2,1)}, bf16[2,1,1,64,5632]{4,3,2,1,0:T(8,128)(2,1)}, u32[]{:S(2)}, u32[]{:S(2)}) collective-permute-start(bf16[2,1,1,64,5632]{4,3,2,1,0:T(8,128)(2,1)} %get-tuple-element.18), channel_id=1, source_target_pairs={{1,0},{2,1},{3,2},{4,3},{5,4},{6,5},{7,6},{8,7},{9,8},{10,9},{11,1... | collective-permute-start | bytes 4325384 | tf_op jit(solution)/shard_map/ppermute | solution.py:17
  228.8 1.9 collective-permute-start
  230.7 52.6 %all-gather.1 = bf16[32,176,9]{1,2,0:T(8,128)(2,1)S(1)} all-gather(bf16[1,176,9]{1,2,0:T(8,128)(2,1)S(1)} %bitcast.35), channel_id=1, replica_groups=mesh['img'=16,'band'=32] {'band'}, dimensions={0}, use_global_device_ids=true | all-gather | bytes 104544 | tf_op jit(solution)/shard_map/all_gather | solution.py:60
  283.3 0.1 copy.26
  283.4 0.3 reshape.139
  283.7 0.6 fusion.20
  284.2 0.0 collective-permute-done.1
  284.2 0.0 collective-permute-done
  284.2 3.8 %fusion.5 = bf16[2,1,4,66,5632]{4,3,2,1,0:T(8,128)(2,1)S(1)} fusion(bf16[2,1,1,64,5632]{4,3,2,1,0:T(8,128)(2,1)} %collective-permute-done.1, bf16[2,1,2,64,5632]{4,3,2,1,0:T(8,128)(2,1)S(1)} %bitcast.28, bf16[2,1,1,64,5632]{4,3,2,1,0:T(8,128)(2,1)} %collective-permute-done), kind=kLoop, calls=%fused_computation.7 | loop fusion | flops 35684352 | bytes 11714560 | tf_op jit(solution)/shard_map/concatenate | solution.py:13
  288.1 6.8 %multiply_add_fusion = f32[2,1,2,64,5632]{4,3,2,1,0:T(8,128)S(1)} fusion(bf16[2,1,2,64,5632]{4,3,2,1,0:T(8,128)(2,1)S(1)} %bitcast.29, bf16[2,1,4,66,5632]{4,3,2,1,0:T(8,128)(2,1)S(1)} %fusion.5, bf16[2,1,1,64,5632]{4,3,2,1,0:T(8,128)(2,1)} %collective-permute-done.1, bf16[2,1,1,64,5632]{4,3,2,1,0:T(8,128)(2,1)} %collective-permute-done, ...), kind=kLoop, calls=%fused_computation.8 | loop fusion | flops 40370176 | bytes 29038592 | tf_op jit(solution)/shard_map/add | solution.py:38
  294.9 0.2 slice_bitcast_fusion
  295.1 0.3 fusion.6
  295.4 1.8 fusion.10
  (10 shorter events, 0.0 us)
Async XLA Ops:
  7.2 62.7 %copy-start.3 = (bf16[176]{0:T(256)(128)(2,1)S(1)}, bf16[176]{0:T(256)(128)(2,1)}, u32[]{:S(2)}) copy-start(bf16[176]{0:T(256)(128)(2,1)} %param.9) | copy-start | bytes 1060
  7.2 63.0 %copy-start.4 = (bf16[176]{0:T(256)(128)(2,1)S(1)}, bf16[176]{0:T(256)(128)(2,1)}, u32[]{:S(2)}) copy-start(bf16[176]{0:T(256)(128)(2,1)} %param.11) | copy-start | bytes 1060
  7.2 202.9 %copy-start = (bf16[1,2,64,1120]{3,2,1,0:T(8,128)(2,1)S(1)}, bf16[1,2,64,1120]{3,2,1,0:T(8,128)(2,1)}, u32[]{:S(2)}) copy-start(bf16[1,2,64,1120]{3,2,1,0:T(8,128)(2,1)} %param.7) | copy-start | bytes 860164
  7.2 202.9 %copy-start.1 = (bf16[1,2,64,1120]{3,2,1,0:T(8,128)(2,1)S(1)}, bf16[1,2,64,1120]{3,2,1,0:T(8,128)(2,1)}, u32[]{:S(2)}) copy-start(bf16[1,2,64,1120]{3,2,1,0:T(8,128)(2,1)} %param.6) | copy-start | bytes 860164
  7.2 203.0 %all-gather.4.cloned.1.call-start = ((), (), s32[]{:S(2)}) async-start(), calls=%async_computation | async-start | bytes 13381632 | tf_op jit(solution)/shard_map/all_gather | solution.py:73
  218.8 11.9 %copy-start.2 = (bf16[9,176]{1,0:T(8,128)(2,1)S(1)}, bf16[9,176]{1,0:T(8,128)(2,1)}, u32[]{:S(2)}) copy-start(bf16[9,176]{1,0:T(8,128)(2,1)} %param.10) | copy-start | bytes 9508
  220.6 63.6 %collective-permute-start.1 = (bf16[2,1,1,64,5632]{4,3,2,1,0:T(8,128)(2,1)}, bf16[2,1,1,64,5632]{4,3,2,1,0:T(8,128)(2,1)}, u32[]{:S(2)}, u32[]{:S(2)}) collective-permute-start(bf16[2,1,1,64,5632]{4,3,2,1,0:T(8,128)(2,1)} %get-tuple-element.18), channel_id=1, source_target_pairs={{1,0},{2,1},{3,2},{4,3},{5,4},{6,5},{7,6},{8,7},{9,8},{10,9},{11,1... | collective-permute-start | bytes 4325384 | tf_op jit(solution)/shard_map/ppermute | solution.py:17
  228.8 55.5 %collective-permute-start = (bf16[2,1,1,64,5632]{4,3,2,1,0:T(8,128)(2,1)}, bf16[2,1,1,64,5632]{4,3,2,1,0:T(8,128)(2,1)}, u32[]{:S(2)}, u32[]{:S(2)}) collective-permute-start(bf16[2,1,1,64,5632]{4,3,2,1,0:T(8,128)(2,1)} %get-tuple-element.17), channel_id=1, source_target_pairs={{0,1},{1,2},{2,3},{3,4},{4,5},{5,6},{6,7},{7,8},{8,9},{9,10},{10,1... | collective-permute-start | bytes 4325384 | tf_op jit(solution)/shard_map/ppermute | solution.py:15
Sparse Core Ops, SparseCore 0:
  68.1 89.3 all-gather.3
where the time goes:
time: 304 us
  blocking collectives  252 us (83%)
  other arithmetic  14.9 us (5%)
  between operations  14.9 us (5%)
  starting transfers between devices  10.1 us (3%)
  matrix products  7.05 us (2%)
  local copies, waits for them, and re-layouts  5.29 us (2%)
    unnamed x1, blocking collectives  140 us
    all_gather x1, blocking collectives, on_device(): weight_rows = lax.all_gather(w_expand, 'img', axis=0, tiled=True)  59.5 us
    all_gather x1, blocking collectives, on_device(): lax.all_gather(w_depth, 'band', axis=1, tiled=True)  52.6 us
    ppermute x1, starting transfers between devices, extended(): lax.ppermute(head, axis, [((i + 1) % count, i) for i in range(ends)])  8.18 us
    dot_general x1, matrix products, on_device(): jnp.dot(stacked, lax.all_gather(weight_rows, 'band', axis=1, tiled=True),...  7.05 us
    add x1, other arithmetic, depthwise(): total + window * depth_taps[3 * row_off + col_off].astype(jnp.float32)  6.78 us
  transfers between devices with their start and end apart: 3, of which 0 were waited for; matrix products, arithmetic and copies ran while one was open for 1% of the time, Pallas kernels for 0%

commit v1 on v0

v1 whole, which is shorter than its diff:
```python
import jax
import jax.numpy as jnp
from jax import lax
from jax.sharding import PartitionSpec as P


def tangent_act(primal_pre, tangent_pre):
    sigmoid_v = jax.nn.sigmoid(primal_pre)
    value = primal_pre * sigmoid_v
    slope = sigmoid_v * (1.0 + primal_pre * (1.0 - sigmoid_v))
    return (value, slope * tangent_pre)


def depthwise(padded, depth_taps, row_count, col_count):
    total = jnp.zeros(padded.shape[:-3] + (row_count, col_count, padded.shape[-1]), jnp.float32)
    for row_off in range(3):
        for col_off in range(3):
            window = padded[
                ..., row_off : row_off + row_count, col_off : col_off + col_count, :
            ].astype(jnp.float32)
            total = total + window * depth_taps[3 * row_off + col_off].astype(jnp.float32)
    return total


def finish(mixed, depth_bias, half):
    primal_mix = mixed[0] + depth_bias.astype(jnp.float32)
    tangent_mix = mixed[1]
    gate_value, gate_tangent = tangent_act(primal_mix[..., half:], tangent_mix[..., half:])
    gated = primal_mix[..., :half] * gate_value
    gated_tangent = tangent_mix[..., :half] * gate_value + primal_mix[..., :half] * gate_tangent
    return (gated.astype(jnp.bfloat16), gated_tangent.astype(jnp.bfloat16))


def on_device(latents, tangents, w_expand, b_expand, w_depth, b_depth):
    row_count, col_count, channels = latents.shape[1:]
    img_count = lax.axis_size("img")
    band_count = lax.axis_size("band")
    band = lax.axis_index("band")
    both = jnp.stack([latents[0], tangents[0]])
    head, tail = both[:, :1], both[:, -1:]
    above = lax.ppermute(tail, "band", [(i, i + 1) for i in range(band_count - 1)])
    below = lax.ppermute(head, "band", [(i + 1, i) for i in range(band_count - 1)])
    small = jnp.concatenate([w_depth, b_expand[None], b_depth[None]], 0)
    small = jnp.pad(small, ((0, img_count - small.shape[0]), (0, 0)))
    mine = lax.dynamic_slice_in_dim(small, lax.axis_index("img"), 1, 0)
    shard = jnp.concatenate([w_expand, mine], 0)
    sent = jnp.broadcast_to(shard[None], (img_count,) + shard.shape)
    blocks = lax.all_to_all(sent, "img", 0, 0)
    depth_rows = w_expand.shape[0]
    columns = jnp.concatenate(
        [blocks[:, :depth_rows].reshape(channels, -1), blocks[:, depth_rows]], 0
    )
    whole = lax.all_gather(columns, "band", axis=1, tiled=True)
    table = whole[channels:]
    full_width = whole.shape[1]
    span_rows = row_count + 2
    span = jnp.concatenate([above, both, below], 1)
    token_count = span_rows * col_count
    stacked = jnp.pad(span.reshape(2 * token_count, channels), ((0, 0), (0, img_count)))
    pre_act = jnp.dot(stacked, whole, preferred_element_type=jnp.float32)
    value, slope_tangent = tangent_act(
        pre_act[:token_count] + table[9].astype(jnp.float32), pre_act[token_count:]
    )
    row = lax.broadcasted_iota(jnp.int32, (token_count, 1), 0) // col_count
    inside = ((row > 0) | (band > 0)) & ((row < span_rows - 1) | (band < band_count - 1))
    activated = jnp.stack(
        [
            jnp.where(inside, value, 0.0).astype(jnp.bfloat16),
            jnp.where(inside, slope_tangent, 0.0).astype(jnp.bfloat16),
        ]
    ).reshape(2, span_rows, col_count, full_width)
    padded = jnp.pad(activated, ((0, 0), (0, 0), (1, 1), (0, 0)))
    mixed = depthwise(padded, table[:9], row_count, col_count)
    gated, gated_tangent = finish(mixed, table[10], full_width // 2)
    return gated[None], gated_tangent[None]


def solution(mesh):
    placed = (
        P("img", "band", None, None),
        P("img", "band", None, None),
        P("img", "band"),
        P("band"),
        P(None, "band"),
        P("band"),
    )
    return jax.shard_map(
        on_device,
        mesh=mesh,
        in_specs=placed,
        out_specs=(P("img", "band", None, None), P("img", "band", None, None)),
        check_vma=False,
    )
```

time: 304 us -> 196 us (0.64)
  blocking collectives: 252 us -> 48.4 us
  waiting for transfers between devices: 0.04 us -> 72.8 us
  other arithmetic: 14.9 us -> 33.7 us
  matrix products: 7.05 us -> 10.5 us
    unnamed x1 -> x0, blocking collectives: 140 us -> none
    all_gather x2 -> x0, blocking collectives: 112 us -> none  [the longest x1 59.5 us: on_device(): weight_rows = lax.all_gather(w_expand, 'img', axis=0, tiled=True)]
    all_gather x1, waiting for transfers between devices: 0.02 us -> 65.2 us  [on_device(): whole = lax.all_gather(columns, 'band', axis=1, tiled=True)]
    all_to_all x0 -> x1, blocking collectives: none -> 48.4 us  [on_device(): blocks = lax.all_to_all(sent, 'img', 0, 0)]
    convert_element_type x1, other arithmetic: 0.01 us -> 14.5 us  [finish(): primal_mix = mixed[0] + depth_bias.astype(jnp.float32)]
    ppermute x2, waiting for transfers between devices: 0.01 us -> 7.53 us  [the longest x1 5.94 us: on_device(): lax.ppermute(head, 'band', [(i + 1, i) for i in range(band_count - 1)])]
    dot_general x1, matrix products: 7.05 us -> 10.5 us  [on_device(): pre_act = jnp.dot(stacked, whole, preferred_element_type=jnp.float32)]
  transfers between devices with their start and end apart: 3 -> 3, of which waited for: 0 -> 3; matrix products, arithmetic and copies ran while one was open for 1% -> 1% of each run, Pallas kernels for 0% -> 0%
where the time goes in v1:
time: 196 us
  waiting for transfers between devices  72.8 us (37%)
  blocking collectives  48.4 us (25%)
  other arithmetic  33.7 us (17%)
  between operations  14.2 us (7%)
  starting transfers between devices  12.8 us (7%)
  matrix products  10.5 us (5%)
  local copies, waits for them, and re-layouts  3.3 us (2%)
    all_gather x1, waiting for transfers between devices, on_device(): whole = lax.all_gather(columns, 'band', axis=1, tiled=True)  65.2 us
    all_to_all x1, blocking collectives, on_device(): blocks = lax.all_to_all(sent, 'img', 0, 0)  48.4 us
    convert_element_type x1, other arithmetic, finish(): primal_mix = mixed[0] + depth_bias.astype(jnp.float32)  14.5 us
    dot_general x1, matrix products, on_device(): pre_act = jnp.dot(stacked, whole, preferred_element_type=jnp.float32)  10.5 us
    add x1, other arithmetic, depthwise(): total + window * depth_taps[3 * row_off + col_off].astype(jnp.float32)  8.17 us
    ppermute x1, starting transfers between devices, on_device(): lax.ppermute(tail, 'band', [(i, i + 1) for i in range(band_count - 1)])  7.61 us
    ppermute x1, waiting for transfers between devices, on_device(): lax.ppermute(head, 'band', [(i + 1, i) for i in range(band_count - 1)])  5.94 us
    convert_element_type x1, other arithmetic, on_device(): jnp.where(inside, value, 0.0).astype(jnp.bfloat16)  5.81 us
  transfers between devices with their start and end apart: 3, of which 3 were waited for; matrix products, arithmetic and copies ran while one was open for 1% of the time, Pallas kernels for 0%

profile of v1, /device:TPU:1, one launch (start us, length us, event | category | flops | bytes accessed | tf_op | source)
XLA Modules:
  0.0 195.7 jit_solution(3714841836156882121)
XLA Ops:
  7.2 0.0 copy-start.1
  7.2 0.0 all-gather.2.cloned.1.call-start
  7.2 0.7 broadcast_in_dim.47
  7.9 0.7 broadcast_in_dim.46
  8.6 0.7 maximum_maximum_fusion
  9.3 0.8 pad_maximum_fusion.3
  10.1 48.4 %all_to_all.5 = bf16[16,71,176]{2,1,0:T(8,128)(2,1)S(1)} all-to-all(bf16[16,71,176]{2,1,0:T(8,128)(2,1)S(1)} %broadcast_in_dim.48), channel_id=1, replica_groups=mesh['img'=16,'band'=32] {'img'}, dimensions={0} | all-to-all | bytes 799744 | tf_op jit(solution)/shard_map/all_to_all | solution.py:48
  58.5 0.1 copy.17
  58.6 0.2 reshape.146
  58.9 0.2 copy.15
  59.1 0.8 pad_maximum_fusion.2
  60.0 0.0 all-gather.2.cloned.1.call-update
  60.0 1.0 constant_dynamic-update-slice_fusion.1
  61.0 0.0 copy-done.1
  61.1 5.2 %collective-permute-start.1 = (bf16[2,1,64,1120]{3,2,1,0:T(8,128)(2,1)S(1)}, bf16[2,1,64,1120]{3,2,1,0:T(8,128)(2,1)S(1)}, u32[]{:S(2)}, u32[]{:S(2)}) collective-permute-start(bf16[2,1,64,1120]{3,2,1,0:T(8,128)(2,1)S(1)} %get-tuple-element.18), channel_id=1, source_target_pairs={{1,0},{2,1},{3,2},{4,3},{5,4},{6,5},{7,6},{8,7},{9,8},{10,9},{11,1... | collective-permute-start | bytes 860168 | tf_op jit(solution)/shard_map/ppermute | solution.py:42
  66.3 7.6 %collective-permute-start = (bf16[2,1,64,1120]{3,2,1,0:T(8,128)(2,1)S(1)}, bf16[2,1,64,1120]{3,2,1,0:T(8,128)(2,1)S(1)}, u32[]{:S(2)}, u32[]{:S(2)}) collective-permute-start(bf16[2,1,64,1120]{3,2,1,0:T(8,128)(2,1)S(1)} %get-tuple-element.17), channel_id=1, source_target_pairs={{0,1},{1,2},{2,3},{3,4},{4,5},{5,6},{6,7},{7,8},{8,9},{9,10},{10,1... | collective-permute-start | bytes 860168 | tf_op jit(solution)/shard_map/ppermute | solution.py:41
  73.9 5.9 %collective-permute-done.1 = bf16[2,1,64,1120]{3,2,1,0:T(8,128)(2,1)S(1)} collective-permute-done((bf16[2,1,64,1120]{3,2,1,0:T(8,128)(2,1)S(1)}, bf16[2,1,64,1120]{3,2,1,0:T(8,128)(2,1)S(1)}, u32[]{:S(2)}, u32[]{:S(2)}) %collective-permute-start.1) | collective-permute-done | bytes 286752 | tf_op jit(solution)/shard_map/ppermute | solution.py:42
  79.9 1.6 collective-permute-done
  81.4 0.2 pad_maximum_fusion.1
  81.6 65.2 %all-gather.2.cloned.1.call-done = bf16[1136,5632]{0,1:T(8,128)(2,1)} async-done(((bf16[1136,176]{0,1:T(8,128)(2,1)}), bf16[1136,5632]{0,1:T(8,128)(2,1)}) %all-gather.2.cloned.1.call-update) | async-done | bytes 12795920 | tf_op jit(solution)/shard_map/all_gather | solution.py:53
  146.8 0.0 copy-start
  146.8 14.5 %convert_reduce_fusion = (f32[5632]{0:T(1024)S(1)}, f32[5632]{0:T(1024)S(1)}, f32[5632]{0:T(1024)S(1)}, f32[5632]{0:T(1024)S(1)}, f32[5632]{0:T(1024)S(1)}, /*in...) fusion(bf16[1136,5632]{0,1:T(8,128)(2,1)} %all-gather.2.cloned., ...), kind=kLoop, calls=%fused_computation.26 | loop fusion | flops 61952 | bytes 371712 | tf_op jit(solution)/shard_map/convert_element_type | solution.py:26
  161.4 0.0 copy-done
  161.4 10.5 %fusion.10 = f32[512,5632]{1,0:T(8,128)} fusion(bf16[1136,5632]{0,1:T(8,128)(2,1)S(1)} %copy-done, bf16[512,1120]{1,0:T(8,128)(2,1)S(1)} %bitcast.22), kind=kOutput, calls=%fused_computation.46 | convolution fusion | flops 6551502848 | bytes 25477120 | tf_op jit(solution)/shard_map/dot_general | solution.py:60
  171.9 5.8 %select_convert_fusion = (bf16[256,5632]{1,0:T(8,128)(2,1)S(1)}, bf16[256,5632]{1,0:T(8,128)(2,1)S(1)}) fusion(f32[512,5632]{1,0:T(8,128)} %fusion.10, f32[5632]{0:T(1024)S(1)} %get-tuple-element.12, pred[256]{0:T(512)(128)(4,1)S(1)} %or_and_fusion), kind=kLoop, calls=%fused_computation.12 | loop fusion | flops 20185088 | bytes 17324288 | tf_op jit(solution)/shard_map/convert_element_type | solution.py:68
  177.7 0.5 pad_maximum_fusion
  178.3 8.2 %multiply_add_fusion = f32[2,2,64,5632]{3,2,1,0:T(8,128)S(1)} fusion(bf16[2,4,64,5632]{3,2,1,0:T(8,128)(2,1)S(1)} %pad_maximum_fusion, bf16[1,4,64,5632]{3,2,1,0:T(8,128)(2,1)S(1)} %bitcast.18, bf16[1,4,64,5632]{3,2,1,0:T(8,128)(2,1)S(1)} %bitcast.20, f32[5632]{0:T(1024)S(1)} %get-tuple-element.3, f32[5632]{0:T(1024)S(1)} %get-tuple-element.4, ...), kind=kLoop, calls=%fused_computation.11 | loop fusion | flops 50462720 | bytes 17504256 | tf_op jit(solution)/shard_map/add | solution.py:21
  186.4 0.2 slice_bitcast_fusion
  186.6 0.3 fusion.5
  186.9 1.9 fusion.13
  (5 shorter events, 0.1 us)
Async XLA Ops:
  7.2 53.8 %copy-start.1 = (bf16[1,2,64,1120]{3,2,1,0:T(8,128)(2,1)S(1)}, bf16[1,2,64,1120]{3,2,1,0:T(8,128)(2,1)}, u32[]{:S(2)}) copy-start(bf16[1,2,64,1120]{3,2,1,0:T(8,128)(2,1)} %param.7) | copy-start | bytes 860164
  7.2 139.7 %all-gather.2.cloned.1.call-start = ((), (), s32[]{:S(2)}) async-start(), calls=%async_computation.1 | async-start | bytes 13381632 | tf_op jit(solution)/shard_map/all_gather | solution.py:53
  61.1 18.8 %collective-permute-start.1 = (bf16[2,1,64,1120]{3,2,1,0:T(8,128)(2,1)S(1)}, bf16[2,1,64,1120]{3,2,1,0:T(8,128)(2,1)S(1)}, u32[]{:S(2)}, u32[]{:S(2)}) collective-permute-start(bf16[2,1,64,1120]{3,2,1,0:T(8,128)(2,1)S(1)} %get-tuple-element.18), channel_id=1, source_target_pairs={{1,0},{2,1},{3,2},{4,3},{5,4},{6,5},{7,6},{8,7},{9,8},{10,9},{11,1... | collective-permute-start | bytes 860168 | tf_op jit(solution)/shard_map/ppermute | solution.py:42
  66.3 15.2 %collective-permute-start = (bf16[2,1,64,1120]{3,2,1,0:T(8,128)(2,1)S(1)}, bf16[2,1,64,1120]{3,2,1,0:T(8,128)(2,1)S(1)}, u32[]{:S(2)}, u32[]{:S(2)}) collective-permute-start(bf16[2,1,64,1120]{3,2,1,0:T(8,128)(2,1)S(1)} %get-tuple-element.17), channel_id=1, source_target_pairs={{0,1},{1,2},{2,3},{3,4},{4,5},{5,6},{6,7},{7,8},{8,9},{9,10},{10,1... | collective-permute-start | bytes 860168 | tf_op jit(solution)/shard_map/ppermute | solution.py:41
  146.8 14.5 %copy-start = (bf16[1136,5632]{0,1:T(8,128)(2,1)S(1)}, bf16[1136,5632]{0,1:T(8,128)(2,1)}, u32[]{:S(2)}) copy-start(bf16[1136,5632]{0,1:T(8,128)(2,1)} %all-gather.2.cloned.1.call-done) | copy-start | bytes 38387716
Sparse Core Ops, SparseCore 0:
  60.1 86.6 all-gather.1

commit v2 on v1

v2 whole, which is shorter than its diff:
```python
import jax
import jax.numpy as jnp
from jax import lax
from jax.experimental import pallas as pl
from jax.experimental.pallas import tpu as pltpu
from jax.sharding import Mesh
from jax.sharding import PartitionSpec as P


LANES = 128
DEPTH = 70
WIDTH = 176
HALF = WIDTH // 2
CORE = 64
REST = HALF - CORE
TAIL = 2 * REST
FOLD = DEPTH // 2
BLOCK = 112
TABLE = DEPTH + FOLD
SPAN = 3
OUT_ROWS = 4
COLS = 64
GROUPS = 6


def ring_pieces(mine, axis):
    up = [(i, (i + 1) % 4) for i in range(4)]
    down = [((i + 1) % 4, i) for i in range(4)]
    cut = mine.shape[0] // 2
    before = lax.ppermute(mine, axis, up)
    after = lax.ppermute(mine, axis, down)
    low = lax.ppermute(before[:cut], axis, up)
    high = lax.ppermute(after[cut:], axis, down)
    return mine, after, low, high, before


def mix_kernel(flag_ref, mine_ref, other_ref, w_ref, table_ref, out_ref, pre_ref, e_ref, m_ref):
    core = flag_ref[2]
    n_part = 2 * SPAN * COLS
    for src, ref in enumerate((mine_ref, other_ref)):
        x = ref[...].reshape(n_part, ref.shape[-1])
        for n in range(GROUPS // 2):
            wide = jnp.dot(
                x, w_ref[:, 2 * n * LANES : 2 * (n + 1) * LANES], preferred_element_type=jnp.float32
            )
            pre_ref[2 * n, pl.ds(src * n_part, n_part), :] = wide[:, :LANES]
            pre_ref[2 * n + 1, pl.ds(src * n_part, n_part), :] = wide[:, LANES:]

    col = lax.broadcasted_iota(jnp.int32, (COLS, LANES), 0)
    lane = lax.broadcasted_iota(jnp.int32, (1, LANES), 1)

    def group(g, carry):
        bias, depth_bias = table_ref[g, pl.ds(9, 1), :], table_ref[g, pl.ds(10, 1), :]
        taps = [table_ref[g, pl.ds(i, 1), :] for i in range(9)]

        def act(r, inner):
            late = r // SPAN
            src = jnp.where(core == 0, late, 1 - late)
            at = pl.multiple_of(src * n_part + (r - SPAN * late) * COLS, COLS)
            p = pre_ref[g, pl.ds(at, COLS), :] + bias
            t = pre_ref[g, pl.ds(at + SPAN * COLS, COLS), :]
            sig = jax.nn.sigmoid(p)
            pair = (p * sig, sig * (1.0 + p * (1.0 - sig)) * t)
            last = jnp.where(r == 2 * SPAN - 1, flag_ref[1], 1)
            inside = jnp.where(r == 0, flag_ref[0], last) > 0
            for k in range(2):
                e = jnp.where(inside, pair[k].astype(jnp.bfloat16).astype(jnp.float32), 0.0)
                e_ref[k, 0, r] = jnp.where(col == 0, 0.0, pltpu.roll(e, 1, 0))
                e_ref[k, 1, r] = e
                e_ref[k, 2, r] = jnp.where(col == COLS - 1, 0.0, pltpu.roll(e, COLS - 1, 0))
            return inner

        def conv(q, inner):
            r = (2 * core + q) % OUT_ROWS
            for k in range(2):
                total = depth_bias if k == 0 else None
                for a in range(3):
                    for b in range(3):
                        term = e_ref[k, b, r + a] * taps[3 * a + b]
                        total = term if total is None else total + term
                m_ref[g, k, q] = total
            return inner

        lax.fori_loop(0, 2 * SPAN, act, 0)
        lax.fori_loop(0, OUT_ROWS, conv, 0)
        return carry

    lax.fori_loop(0, GROUPS, group, 0)

    def gated(q, to, split):
        (vp, gp), (vt, gt) = split(0), split(1)
        sig = jax.nn.sigmoid(gp)
        gate = gp * sig
        gate_t = sig * (1.0 + gp * (1.0 - sig)) * gt
        out_ref[q, to, 0] = (vp * gate).astype(jnp.bfloat16)
        out_ref[q, to, 1] = (vt * gate + vp * gate_t).astype(jnp.bfloat16)

    def rows(q, carry):
        for pair in range(2):

            def split(k, pair=pair):
                a, b = m_ref[2 * pair, k, q], m_ref[2 * pair + 1, k, q]
                value = jnp.where(lane < CORE, a, pltpu.roll(b, CORE, 1))
                return value, jnp.where(lane < CORE, pltpu.roll(a, CORE, 1), b)

            gated(q, pair, split)
        here = (lane < REST) | ((lane >= TAIL) & (lane < TAIL + REST))

        def split_tail(k):
            a, b = m_ref[4, k, q], m_ref[5, k, q]
            value = jnp.where(here, a, pltpu.roll(b, REST, 1))
            return value, jnp.where(here, pltpu.roll(a, LANES - REST, 1), b)

        gated(q, 2, split_tail)
        return carry

    lax.fori_loop(0, OUT_ROWS, rows, 0)


def mix(flags, mine, others, weights, table, slot):
    whole = pl.BlockSpec(memory_space=pltpu.VMEM)
    part = pl.BlockSpec((1,) + mine.shape[1:], lambda i: (slot, 0, 0, 0, 0))
    n_tok = 4 * SPAN * COLS
    return pl.pallas_call(
        mix_kernel,
        grid=(1,),
        out_shape=jax.ShapeDtypeStruct((OUT_ROWS, 3, 2, COLS, LANES), jnp.bfloat16),
        in_specs=[pl.BlockSpec(memory_space=pltpu.SMEM), part, part, whole, whole],
        out_specs=whole,
        scratch_shapes=[
            pltpu.VMEM((GROUPS, n_tok, LANES), jnp.float32),
            pltpu.VMEM((2, 3, 2 * SPAN, COLS, LANES), jnp.float32),
            pltpu.VMEM((GROUPS, 2, OUT_ROWS, COLS, LANES), jnp.float32),
        ],
        cost_estimate=pl.CostEstimate(
            flops=2 * n_tok * weights.size, bytes_accessed=5_000_000, transcendentals=1_000_000
        ),
    )(flags, mine, others, weights, table)


def weave_kernel(flag_ref, keep_ref, take_ref, *out):
    mine_first = flag_ref[0] == 0
    y = flag_ref[1]
    lane = lax.broadcasted_iota(jnp.int32, (1, LANES), 1)

    def row(r, carry):
        for k in range(2):
            segments = []
            for source in range(4):
                at = (source - y + 4) % 4
                groups = []
                for g in range(3):
                    own = keep_ref[at, r, g, k].astype(jnp.float32)
                    other = take_ref[at, r, g, k].astype(jnp.float32)
                    groups.append(
                        (jnp.where(mine_first, own, other), jnp.where(mine_first, other, own))
                    )
                for zl in range(4):
                    for core in range(2):
                        start = WIDTH * (8 * (source % 2) + 2 * zl + core) + HALF * (source // 2)
                        odd, pair = zl % 2, zl // 2
                        segments.append((start, CORE * odd, CORE, groups[pair][core]))
                        lanes = TAIL * odd + REST * pair
                        segments.append((start + CORE, lanes, REST, groups[2][core]))
            for n in range(16 * WIDTH // LANES):
                tile = None
                for start, first, count, block in segments:
                    lo, hi = start - n * LANES, start + count - n * LANES
                    if hi <= 0 or lo >= LANES:
                        continue
                    shift = (lo - first) % LANES
                    moved = pltpu.roll(block, shift, 1) if shift else block
                    if tile is None:
                        tile = moved
                    else:
                        tile = jnp.where((lane >= lo) & (lane < hi), moved, tile)
                out[k][0, r, :, pl.ds(n * LANES, LANES)] = tile.astype(jnp.bfloat16)
        return carry

    lax.fori_loop(0, 2, row, 0)


def weave(flags, keep, take):
    out = jax.ShapeDtypeStruct((1, 2, COLS, 16 * WIDTH), jnp.bfloat16)
    whole = pl.BlockSpec(memory_space=pltpu.VMEM)
    return pl.pallas_call(
        weave_kernel,
        out_shape=(out, out),
        in_specs=[pl.BlockSpec(memory_space=pltpu.SMEM)] + [whole] * 2,
        out_specs=(whole, whole),
    )(flags, keep, take)


def on_device(latents, tangents, w_expand, b_expand, w_depth, b_depth):
    channels = latents.shape[-1]
    core, x, y = lax.axis_index("core"), lax.axis_index("x"), lax.axis_index("y")
    zl = lax.axis_index("zl")
    across = [(0, 1), (1, 0)]
    small = jnp.concatenate([w_depth, b_expand[None], b_depth[None], jnp.zeros_like(b_depth)[None]], 0)
    three = lax.dynamic_slice_in_dim(small, 3 * lax.axis_index("zh"), 3, 0)
    shard = jnp.concatenate([w_expand, three], 0)
    front = y < 2
    low, high = shard[:, :HALF], shard[:, HALF:]
    got = lax.ppermute(jnp.where(front, high, low), "y", [(i, (i + 2) % 4) for i in range(4)])
    held = jnp.where(front, low, high)
    value, gate = jnp.where(front, held, got), jnp.where(front, got, held)
    zeros = lambda rows, lanes: jnp.zeros((rows, lanes), w_expand.dtype)
    main = jnp.concatenate([value[:, :CORE], gate[:, :CORE]], 1)
    tail = jnp.concatenate([value[:, CORE:], gate[:, CORE:]], 1)
    block = jnp.concatenate(
        [
            main[:DEPTH],
            jnp.concatenate([tail[:FOLD], tail[FOLD:DEPTH], zeros(FOLD, LANES - 2 * TAIL)], 1),
            main[DEPTH:],
            jnp.concatenate([tail[DEPTH:], zeros(3, LANES - TAIL)], 1),
            zeros(1, LANES),
        ],
        0,
    )
    sent = jnp.broadcast_to(block[None], (16,) + block.shape)
    column = lax.all_to_all(sent, ("zh", "zl"), 0, 0)

    edge = jnp.where(
        core == 0,
        jnp.concatenate([latents[:, 0], tangents[:, 0]], 0),
        jnp.concatenate([latents[:, -1], tangents[:, -1]], 0),
    )
    near = [(2 * q + 1, 2 * q + 2) for q in range(15)]
    beyond = lax.ppermute(edge, ("y", "zl", "core"), near + [(b, a) for a, b in near])
    rows = [jnp.concatenate([latents[:, r], tangents[:, r]], 0) for r in range(2)]
    mine = jnp.stack(
        [
            jnp.where(core == 0, beyond, rows[0]),
            jnp.where(core == 0, rows[0], rows[1]),
            jnp.where(core == 0, rows[1], beyond),
        ],
        1,
    )
    own, after, low, high, before = ring_pieces(mine, "y")
    mine = jnp.stack([own, after, jnp.concatenate([low, high], 0), before])
    others = lax.ppermute(mine, "core", across)

    own, after, low, high, before = ring_pieces(column, "x")
    turned = jnp.concatenate([own, after, low, high, before], 0).reshape(4, 4, 4, BLOCK, LANES)
    turned = jnp.concatenate([turned, turned[:3]], 0)
    ordered = lax.dynamic_slice_in_dim(turned, (4 - x) % 4, 4, 0).reshape(16, 4, BLOCK, LANES)
    first = ordered[:, :, :DEPTH].transpose(0, 2, 1, 3).reshape(channels, 4 * LANES)
    folded = ordered[:, :, DEPTH:TABLE]
    second = jnp.concatenate([folded[..., :TAIL], folded[..., TAIL : 2 * TAIL]], 2)
    tails = lambda t, n: jnp.pad(
        t.transpose(0, 2, 1, 3).reshape(n, 2, 2 * TAIL), ((0, 0), (0, 0), (0, LANES - 2 * TAIL))
    )
    weights = jnp.concatenate([first, tails(second, channels).reshape(channels, 2 * LANES)], 1)
    extra = ordered[:4, :, TABLE : TABLE + 6]
    table = jnp.concatenate(
        [
            extra[:, :, :3].transpose(0, 2, 1, 3).reshape(12, 4, LANES),
            tails(extra[:, :, 3:, :TAIL], 12),
        ],
        1,
    ).transpose(1, 0, 2).astype(jnp.float32)

    results = {}
    for turn in (2, 1, 3, 0):
        chip = 4 * ((y + turn) % 4) + zl
        flags = jnp.stack([(chip > 0).astype(jnp.int32), (chip < 15).astype(jnp.int32), core])
        done = mix(flags, mine, others, weights, table, turn)
        if turn:
            done = lax.ppermute(done, "y", [(i, (i + turn) % 4) for i in range(4)])
        results[(4 - turn) % 4] = done
    keep = jnp.stack([results[i] for i in range(4)])
    give = jnp.stack([results[i][2:] for i in range(4)])
    take = lax.ppermute(give, "core", across)
    return weave(jnp.stack([core, y]), keep, take)


def solution(mesh):
    split = Mesh(mesh.devices.reshape(4, 4, 4, 4, 2), ("x", "zh", "y", "zl", "core"))
    img, band = ("x", "zh"), ("y", "zl", "core")
    placed = (
        P(img, band, None, None),
        P(img, band, None, None),
        P(img, band),
        P(band),
        P(None, band),
        P(band),
    )

    return jax.shard_map(
        on_device,
        mesh=split,
        in_specs=placed,
        out_specs=(P(img, band, None, None), P(img, band, None, None)),
        check_vma=False,
    )
```

time: 196 us -> 198 us (1.010)
  starting transfers between devices: 12.8 us -> 72.5 us
  blocking collectives: 48.4 us -> 0 us
  Pallas kernels: 0 us -> 35.9 us
  waiting for transfers between devices: 72.8 us -> 43.6 us
  local copies, waits for them, and re-layouts: 3.3 us -> 26.9 us
  other arithmetic: 33.7 us -> 16.6 us
  between operations: 14.2 us -> 1.22 us
  matrix products: 10.5 us -> 0 us
    all_gather x1 -> x0, waiting for transfers between devices: 65.2 us -> none  [on_device(): whole = lax.all_gather(columns, 'band', axis=1, tiled=True)]
    all_to_all x1 -> x0, blocking collectives: 48.4 us -> none  [on_device(): blocks = lax.all_to_all(sent, 'img', 0, 0)]
    ppermute x2 -> x15, starting transfers between devices: 12.8 us -> 54.1 us  [the longest x1 8.93 us: on_device(): take = lax.ppermute(give, 'core', across)]
    pallas_call x0 -> x5, Pallas kernels: none -> 35.9 us  [the longest x4 32 us: mix(): pl.pallas_call(mix_kernel, grid=(1,), out_shape=jax.ShapeDtypeStruct((OUT...]
    ppermute x2 -> x15, waiting for transfers between devices: 7.53 us -> 27.9 us  [the longest x1 13.8 us: on_device(): lax.ppermute(jnp.where(front, high, low), 'y', [(i, (i + 2) % 4) for i in...]
    convert_element_type x2 -> x1, other arithmetic: 20.3 us -> 1.32 us  [on_device(): table = jnp.concatenate([extra[:, :, :3].transpose(0, 2, 1, 3).reshape(12...]
    all_to_all x0 -> x1, starting transfers between devices: none -> 18.4 us  [on_device(): column = lax.all_to_all(sent, ('zh', 'zl'), 0, 0)]
    all_to_all x0 -> x1, waiting for transfers between devices: none -> 15.7 us  [on_device(): column = lax.all_to_all(sent, ('zh', 'zl'), 0, 0)]
  transfers between devices with their start and end apart: 3 -> 16, of which waited for: 3 -> 7; matrix products, arithmetic and copies ran while one was open for 1% -> 20% of each run, Pallas kernels for 0% -> 12%
where the time goes in v2:
time: 198 us; the launch traced here: 197 us
  starting transfers between devices  72.5 us (37%)
  waiting for transfers between devices  43.6 us (22%)
  Pallas kernels  35.9 us (18%)
  local copies, waits for them, and re-layouts  26.9 us (14%)
  other arithmetic  16.6 us (8%)
    pallas_call x4, Pallas kernels, mix(): pl.pallas_call(mix_kernel, grid=(1,), out_shape=jax.ShapeDtypeStruct((OUT...  32 us
    all_to_all x1, starting transfers between devices, on_device(): column = lax.all_to_all(sent, ('zh', 'zl'), 0, 0)  18.4 us
    all_to_all x1, waiting for transfers between devices, on_device(): column = lax.all_to_all(sent, ('zh', 'zl'), 0, 0)  15.7 us
    ppermute x1, waiting for transfers between devices, on_device(): lax.ppermute(jnp.where(front, high, low), 'y', [(i, (i + 2) % 4) for i in...  13.8 us
    ppermute x1, starting transfers between devices, on_device(): take = lax.ppermute(give, 'core', across)  8.93 us
    ppermute x3, starting transfers between devices, on_device(): done = lax.ppermute(done, 'y', [(i, (i + turn) % 4) for i in range(4)])  7.94 us
    ppermute x2, starting transfers between devices, ring_pieces(): after = lax.ppermute(mine, axis, down)  7.09 us
    ppermute x2, starting transfers between devices, ring_pieces(): high = lax.ppermute(after[cut:], axis, down)  6.48 us
  transfers between devices with their start and end apart: 16, of which 7 were waited for; matrix products, arithmetic and copies ran while one was open for 20% of the time, Pallas kernels for 12%

profile of v2, /device:TPU:1, one launch (start us, length us, event | category | flops | bytes accessed | tf_op | source)
XLA Modules:
  0.0 196.8 jit_solution(13565381204155592107)
XLA Ops:
  2.0 4.9 %collective-permute-start = (bf16[2,64,1120]{2,1,0:T(8,128)(2,1)S(1)}, bf16[2,64,1120]{2,1,0:T(8,128)(2,1)S(1)}, u32[]{:S(2)}, u32[]{:S(2)}) collective-permute-start(bf16[2,64,1120]{2,1,0:T(8,128)(2,1)S(1)} %broadcast_select_fusion), channel_id=1, source_target_pairs={{1,2},{3,4},{5,6},{7,8},{9,10},{11,12},{13,14},{15,16},{17,18},{19... | collective-permute-start | bytes 860168 | tf_op jit(solution)/shard_map/ppermute | solution.py:229
  7.2 5.3 %collective-permute-done = bf16[2,64,1120]{2,1,0:T(8,128)(2,1)S(1)} collective-permute-done((bf16[2,64,1120]{2,1,0:T(8,128)(2,1)S(1)}, bf16[2,64,1120]{2,1,0:T(8,128)(2,1)S(1)}, u32[]{:S(2)}, u32[]{:S(2)}) %collective-permute-start) | collective-permute-done | bytes 286752 | tf_op jit(solution)/shard_map/ppermute | solution.py:229
  13.7 3.7 %collective-permute-start.1 = (bf16[2,3,64,1120]{3,2,1,0:T(8,128)(2,1)S(1)}, bf16[2,3,64,1120]{3,2,1,0:T(8,128)(2,1)S(1)}, u32[]{:S(2)}, u32[]{:S(2)}) collective-permute-start(bf16[2,3,64,1120]{3,2,1,0:T(8,128)(2,1)S(1)} %get-tuple-element.5), channel_id=1, source_target_pairs={{8,0},{16,8},{24,16},{0,24},{9,1},{17,9},{25,17},{1,25},{10,2},{18... | collective-permute-start | bytes 2580488 | tf_op jit(solution)/shard_map/ppermute | solution.py:31
  17.4 1.9 collective-permute-start.2
  19.5 5.3 %collective-permute-start.6 = (bf16[73,88]{1,0:T(8,128)(2,1)S(1)}, bf16[73,88]{1,0:T(8,128)(2,1)S(1)}, u32[]{:S(2)}, u32[]{:S(2)}) collective-permute-start(bf16[73,88]{1,0:T(8,128)(2,1)S(1)} %broadcast_select_fusion.3), channel_id=1, source_target_pairs={{0,16},{8,24},{16,0},{24,8},{1,17},{9,25},{17,1},{25,9},{2,18},{10... | collective-permute-start | bytes 38552 | tf_op jit(solution)/shard_map/ppermute | solution.py:204
  24.9 13.8 %collective-permute-done.6 = bf16[73,88]{1,0:T(8,128)(2,1)S(1)} collective-permute-done((bf16[73,88]{1,0:T(8,128)(2,1)S(1)}, bf16[73,88]{1,0:T(8,128)(2,1)S(1)}, u32[]{:S(2)}, u32[]{:S(2)}) %collective-permute-start.6) | collective-permute-done | bytes 12880 | tf_op jit(solution)/shard_map/ppermute | solution.py:204
  40.8 1.9 collective-permute-start.4
  42.7 3.4 %collective-permute-start.3 = (bf16[1,3,64,1120]{3,2,1,0:T(8,128)(2,1)S(1)}, bf16[1,3,64,1120]{3,2,1,0:T(8,128)(2,1)S(1)}, u32[]{:S(2)}, u32[]{:S(2)}) collective-permute-start(bf16[1,3,64,1120]{3,2,1,0:T(8,128)(2,1)S(1)} %slice.128), channel_id=1, source_target_pairs={{0,8},{8,16},{16,24},{24,0},{1,9},{9,17},{17,25},{25,1},{2,10},{10... | collective-permute-start | bytes 1290248 | tf_op jit(solution)/shard_map/ppermute | solution.py:32
  47.9 18.4 %all-to-all-start = ((bf16[16,112,128]{2,1,0:T(8,128)(2,1)}), bf16[16,112,128]{2,1,0:T(8,128)(2,1)}, u32[]{:S(2)}, u32[]{:S(2)}) async-start(bf16[16,112,128]{2,1,0:T(8,128)(2,1)} %broadcast_in_dim.23), calls=%async_computation | async-start | bytes 917504 | tf_op jit(solution)/shard_map/all_to_all | solution.py:221
  66.4 2.0 %pad_maximum_fusion.mine_ref = bf16[4,2,3,64,1120]{4,3,2,1,0:T(8,128)(2,1)S(1)} fusion(bf16[1,2,3,64,1120]{4,3,2,1,0:T(8,128)(2,1)} %bitcast.80, bf16[1,2,3,64,1120]{4,3,2,1,0:T(8,128)(2,1)S(1)} %maximum_bitcast_fusion.1, bf16[1,2,3,64,1120]{4,3,2,1,0:T(8,128)(2,1)} %bitcast.79, bf16[1,2,3,64,1120]{4,3,2,1,0:T(8,128)(2,1)} %get-tuple-element.4), kind=kLoop, calls=%fused_computation | loop fusion | flops 5160960 | bytes 6881280 | tf_op jit(solution)/shard_map/stack | solution.py:240
  68.5 3.1 %collective-permute-start.5 = (bf16[4,2,3,64,1120]{4,3,2,1,0:T(8,128)(2,1)S(1)}, bf16[4,2,3,64,1120]{4,3,2,1,0:T(8,128)(2,1)}, u32[]{:S(2)}, u32[]{:S(2)}) collective-permute-start(bf16[4,2,3,64,1120]{4,3,2,1,0:T(8,128)(2,1)S(1)} %pad_maximum_fusion.mine_ref), channel_id=1, source_target_pairs={{0,1},{1,0},{2,3},{3,2},{4,5},{5,4},{6,7},{7,6},{8,9},{9,8},{10,11... | collective-permute-start | bytes 10321928 | tf_op jit(solution)/shard_map/ppermute | solution.py:241
  71.5 15.7 %all-to-all-done = bf16[16,112,128]{2,1,0:T(8,128)(2,1)} async-done(((bf16[16,112,128]{2,1,0:T(8,128)(2,1)}), bf16[16,112,128]{2,1,0:T(8,128)(2,1)}, u32[]{:S(2)}, u32[]{:S(2)}) %all-to-all-start) | async-done | bytes 458784 | tf_op jit(solution)/shard_map/all_to_all | solution.py:221
  87.3 3.1 %collective-permute-start.8 = (bf16[16,112,128]{2,1,0:T(8,128)(2,1)}, bf16[16,112,128]{2,1,0:T(8,128)(2,1)}, u32[]{:S(2)}, u32[]{:S(2)}) collective-permute-start(bf16[16,112,128]{2,1,0:T(8,128)(2,1)} %all-to-all-done), channel_id=1, source_target_pairs={{0,128},{128,256},{256,384},{384,0},{1,129},{129,257},{257,385},{3... | collective-permute-start | bytes 1376264 | tf_op jit(solution)/shard_map/ppermute | solution.py:30
  91.1 3.4 %collective-permute-start.7 = (bf16[16,112,128]{2,1,0:T(8,128)(2,1)}, bf16[16,112,128]{2,1,0:T(8,128)(2,1)S(1)}, u32[]{:S(2)}, u32[]{:S(2)}) collective-permute-start(bf16[16,112,128]{2,1,0:T(8,128)(2,1)} %all-to-all-done), channel_id=1, source_target_pairs={{128,0},{256,128},{384,256},{0,384},{129,1},{257,129},{385,257},{1... | collective-permute-start | bytes 1376264 | tf_op jit(solution)/shard_map/ppermute | solution.py:31
  99.0 1.9 collective-permute-start.9
  102.0 4.6 %collective-permute-start.10 = (bf16[8,112,128]{2,1,0:T(8,128)(2,1)S(1)}, bf16[8,112,128]{2,1,0:T(8,128)(2,1)S(1)}, u32[]{:S(2)}, u32[]{:S(2)}) collective-permute-start(bf16[8,112,128]{2,1,0:T(8,128)(2,1)S(1)} %slice.143), channel_id=1, source_target_pairs={{128,0},{256,128},{384,256},{0,384},{129,1},{257,129},{385,257},{1... | collective-permute-start | bytes 688136 | tf_op jit(solution)/shard_map/ppermute | solution.py:33
  107.6 2.9 %collective-permute-done.10 = bf16[8,112,128]{2,1,0:T(8,128)(2,1)S(1)} collective-permute-done((bf16[8,112,128]{2,1,0:T(8,128)(2,1)S(1)}, bf16[8,112,128]{2,1,0:T(8,128)(2,1)S(1)}, u32[]{:S(2)}, u32[]{:S(2)}) %collective-permute-start.10) | collective-permute-done | bytes 229408 | tf_op jit(solution)/shard_map/ppermute | solution.py:33
  123.1 2.6 %copy.17 = bf16[16,70,4,48]{1,0,3,2:T(8,128)(2,1)} copy(bf16[16,70,4,48]{3,1,2,0:T(8,128)(2,1)} %maximum_bitcast_fusion) | data formatting | bytes 860160 | tf_op jit(solution)/shard_map/transpose | solution.py:251
  125.8 2.6 %reshape.77 = bf16[1120,2,96]{0,2,1:T(8,128)(2,1)} reshape(bf16[16,70,4,48]{1,0,3,2:T(8,128)(2,1)} %copy.17) | data formatting | bytes 860160 | tf_op jit(solution)/shard_map/reshape | solution.py:251
  128.4 1.9 pad.9
  130.3 2.1 %copy.23 = bf16[1120,256]{1,0:T(8,128)(2,1)} copy(bf16[1120,256]{0,1:T(8,128)(2,1)} %bitcast.78) | data formatting | bytes 1146880 | tf_op jit(solution)/shard_map/reshape | solution.py:253
  133.7 2.8 %pad_maximum_fusion.1.w_ref = bf16[1120,768]{1,0:T(8,128)(2,1)} fusion(bf16[1120,256]{1,0:T(8,128)(2,1)} %copy.23, bf16[1120,512]{1,0:T(8,128)(2,1)} %bitcast.75), kind=kLoop, calls=%fused_computation.4 | loop fusion | flops 3440640 | bytes 3440640 | tf_op jit(solution)/shard_map/concatenate | solution.py:253
  136.5 8.0 %shard_map.78 = bf16[4,3,2,64,128]{4,3,2,1,0:T(8,128)(2,1)} custom-call(s32[3]{0:T(128)} %add_add_fusion.1.flag_ref, bf16[4,2,3,64,1120]{4,3,2,1,0:T(8,128)(2,1)} %copy-done, bf16[4,2,3,64,1120]{4,3,2,1,0:T(8,128)(2,1)} %collective-permute-done.5.other_ref, bf16[1120,768]{1,0:T(8,128)(2,1)} %pad_maximum_fusion.1.w_ref, ...), custom_call_target="tpu_custom_call" | custom-call | flops 1321205760 | bytes 5000000 | tf_op jit(solution)/shard_map/pallas_call | solution.py:124
  144.5 3.4 %collective-permute-start.11 = (bf16[4,3,2,64,128]{4,3,2,1,0:T(8,128)(2,1)}, bf16[4,3,2,64,128]{4,3,2,1,0:T(8,128)(2,1)S(1)}, u32[]{:S(2)}, u32[]{:S(2)}) collective-permute-start(bf16[4,3,2,64,128]{4,3,2,1,0:T(8,128)(2,1)} %shard_map.78), channel_id=1, source_target_pairs={{0,24},{8,0},{16,8},{24,16},{1,25},{9,1},{17,9},{25,17},{2,26},{10... | collective-permute-start | bytes 1179656 | tf_op jit(solution)/shard_map/ppermute | solution.py:269
  147.9 8.0 %shard_map.79 = bf16[4,3,2,64,128]{4,3,2,1,0:T(8,128)(2,1)} custom-call(s32[3]{0:T(128)} %add_add_fusion.2.flag_ref, bf16[4,2,3,64,1120]{4,3,2,1,0:T(8,128)(2,1)} %copy-done, bf16[4,2,3,64,1120]{4,3,2,1,0:T(8,128)(2,1)} %collective-permute-done.5.other_ref, bf16[1120,768]{1,0:T(8,128)(2,1)} %pad_maximum_fusion.1.w_ref, ...), custom_call_target="tpu_custom_call" | custom-call | flops 1321205760 | bytes 5000000 | tf_op jit(solution)/shard_map/pallas_call | solution.py:124
  155.9 2.7 %collective-permute-start.12 = (bf16[4,3,2,64,128]{4,3,2,1,0:T(8,128)(2,1)}, bf16[4,3,2,64,128]{4,3,2,1,0:T(8,128)(2,1)S(1)}, u32[]{:S(2)}, u32[]{:S(2)}) collective-permute-start(bf16[4,3,2,64,128]{4,3,2,1,0:T(8,128)(2,1)} %shard_map.79), channel_id=1, source_target_pairs={{0,16},{8,24},{16,0},{24,8},{1,17},{9,25},{17,1},{25,9},{2,18},{10... | collective-permute-start | bytes 1179656 | tf_op jit(solution)/shard_map/ppermute | solution.py:269
  158.6 8.0 %shard_map.80 = bf16[4,3,2,64,128]{4,3,2,1,0:T(8,128)(2,1)} custom-call(s32[3]{0:T(128)} %add_add_fusion.3.flag_ref, bf16[4,2,3,64,1120]{4,3,2,1,0:T(8,128)(2,1)} %copy-done, bf16[4,2,3,64,1120]{4,3,2,1,0:T(8,128)(2,1)} %collective-permute-done.5.other_ref, bf16[1120,768]{1,0:T(8,128)(2,1)} %pad_maximum_fusion.1.w_ref, ...), custom_call_target="tpu_custom_call" | custom-call | flops 1321205760 | bytes 5000000 | tf_op jit(solution)/shard_map/pallas_call | solution.py:124
  166.6 1.9 collective-permute-start.13
  168.5 8.0 %shard_map.77 = bf16[4,3,2,64,128]{4,3,2,1,0:T(8,128)(2,1)} custom-call(s32[3]{0:T(128)} %add_add_fusion.flag_ref, bf16[4,2,3,64,1120]{4,3,2,1,0:T(8,128)(2,1)} %copy-done, bf16[4,2,3,64,1120]{4,3,2,1,0:T(8,128)(2,1)} %collective-permute-done.5.other_ref, bf16[1120,768]{1,0:T(8,128)(2,1)} %pad_maximum_fusion.1.w_ref, f32[6,12,128]{2,1,0:T(8,128)} %convert_bitcast_fusion.table_ref), custom_call_target="tpu_custom_call" | custom-call | flops 1321205760 | bytes 5000000 | tf_op jit(solution)/shard_map/pallas_call | solution.py:124
  177.6 3.3 %collective-permute-done.13 = bf16[4,3,2,64,128]{4,3,2,1,0:T(8,128)(2,1)S(1)} collective-permute-done((bf16[4,3,2,64,128]{4,3,2,1,0:T(8,128)(2,1)}, bf16[4,3,2,64,128]{4,3,2,1,0:T(8,128)(2,1)S(1)}, u32[]{:S(2)}, u32[]{:S(2)}) %collective-permute-start.13) | collective-permute-done | bytes 393248 | tf_op jit(solution)/shard_map/ppermute | solution.py:269
  181.0 8.9 %collective-permute-start.14 = (bf16[4,2,3,2,64,128]{5,4,3,2,1,0:T(8,128)(2,1)S(1)}, bf16[4,2,3,2,64,128]{5,4,3,2,1,0:T(8,128)(2,1)S(1)}, u32[]{:S(2)}, u32[]{:S(2)}) collective-permute-start(bf16[4,2,3,2,64,128]{5,4,3,2,1,0:T(8,128)(2,1)S(1)} %pad_maximum_fusion.5), channel_id=1, source_target_pairs={{0,1},{1,0},{2,3},{3,2},{4,5},{5,4},{6,7},{7,6},{8,9},{9,8},{10,11... | collective-permute-start | bytes 2359304 | tf_op jit(solution)/shard_map/ppermute | solution.py:273
  192.9 3.9 %shard_map.81 = (bf16[1,2,64,2816]{3,2,1,0:T(8,128)(2,1)}, bf16[1,2,64,2816]{3,2,1,0:T(8,128)(2,1)}) custom-call(s32[2]{0:T(128)} %pad_add_fusion.flag_ref, bf16[4,4,3,2,64,128]{5,4,3,2,1,0:T(8,128)(2,1)} %pad_maximum_fusion.2.keep_ref, bf16[4,2,3,2,64,128]{5,4,3,2,1,0:T(8,128)(2,1)} %copy-done.6), custom_call_target="tpu_custom_call" | custom-call | tf_op jit(solution)/shard_map/pallas_call | solution.py:186
  (92 shorter events, 32.1 us)
Async XLA Ops:
  0.6 6.3 %copy-start.9 = (bf16[176]{0:T(256)(128)(2,1)S(1)}, bf16[176]{0:T(256)(128)(2,1)}, u32[]{:S(2)}) copy-start(bf16[176]{0:T(256)(128)(2,1)} %param.9) | copy-start | bytes 1060
  0.6 6.3 %copy-start.10 = (bf16[176]{0:T(256)(128)(2,1)S(1)}, bf16[176]{0:T(256)(128)(2,1)}, u32[]{:S(2)}) copy-start(bf16[176]{0:T(256)(128)(2,1)} %param.11) | copy-start | bytes 1060
  2.0 10.5 %collective-permute-start = (bf16[2,64,1120]{2,1,0:T(8,128)(2,1)S(1)}, bf16[2,64,1120]{2,1,0:T(8,128)(2,1)S(1)}, u32[]{:S(2)}, u32[]{:S(2)}) collective-permute-start(bf16[2,64,1120]{2,1,0:T(8,128)(2,1)S(1)} %broadcast_select_fusion), channel_id=1, source_target_pairs={{1,2},{3,4},{5,6},{7,8},{9,10},{11,12},{13,14},{15,16},{17,18},{19... | collective-permute-start | bytes 860168 | tf_op jit(solution)/shard_map/ppermute | solution.py:229
  7.2 12.1 %copy-start.8 = (bf16[9,176]{1,0:T(8,128)(2,1)S(1)}, bf16[9,176]{1,0:T(8,128)(2,1)}, u32[]{:S(2)}) copy-start(bf16[9,176]{1,0:T(8,128)(2,1)} %param.10) | copy-start | bytes 9508
  7.2 12.2 %copy-start.7 = (bf16[70,176]{1,0:T(8,128)(2,1)S(1)}, bf16[70,176]{1,0:T(8,128)(2,1)}, u32[]{:S(2)}) copy-start(bf16[70,176]{1,0:T(8,128)(2,1)} %param.8) | copy-start | bytes 73924
  13.7 26.2 %collective-permute-start.1 = (bf16[2,3,64,1120]{3,2,1,0:T(8,128)(2,1)S(1)}, bf16[2,3,64,1120]{3,2,1,0:T(8,128)(2,1)S(1)}, u32[]{:S(2)}, u32[]{:S(2)}) collective-permute-start(bf16[2,3,64,1120]{3,2,1,0:T(8,128)(2,1)S(1)} %get-tuple-element.5), channel_id=1, source_target_pairs={{8,0},{16,8},{24,16},{0,24},{9,1},{17,9},{25,17},{1,25},{10,2},{18... | collective-permute-start | bytes 2580488 | tf_op jit(solution)/shard_map/ppermute | solution.py:31
  17.4 25.2 %collective-permute-start.2 = (bf16[2,3,64,1120]{3,2,1,0:T(8,128)(2,1)S(1)}, bf16[2,3,64,1120]{3,2,1,0:T(8,128)(2,1)S(1)}, u32[]{:S(2)}, u32[]{:S(2)}) collective-permute-start(bf16[2,3,64,1120]{3,2,1,0:T(8,128)(2,1)S(1)} %get-tuple-element.5), channel_id=1, source_target_pairs={{0,8},{8,16},{16,24},{24,0},{1,9},{9,17},{17,25},{25,1},{2,10},{10... | collective-permute-start | bytes 2580488 | tf_op jit(solution)/shard_map/ppermute | solution.py:30
  19.5 19.2 %collective-permute-start.6 = (bf16[73,88]{1,0:T(8,128)(2,1)S(1)}, bf16[73,88]{1,0:T(8,128)(2,1)S(1)}, u32[]{:S(2)}, u32[]{:S(2)}) collective-permute-start(bf16[73,88]{1,0:T(8,128)(2,1)S(1)} %broadcast_select_fusion.3), channel_id=1, source_target_pairs={{0,16},{8,24},{16,0},{24,8},{1,17},{9,25},{17,1},{25,9},{2,18},{10... | collective-permute-start | bytes 38552 | tf_op jit(solution)/shard_map/ppermute | solution.py:204
  39.9 26.6 %copy-start.4 = (bf16[2,3,64,1120]{3,2,1,0:T(8,128)(2,1)}, bf16[2,3,64,1120]{3,2,1,0:T(8,128)(2,1)S(1)}, u32[]{:S(2)}) copy-start(bf16[2,3,64,1120]{3,2,1,0:T(8,128)(2,1)S(1)} %collective-permute-done.1) | copy-start | bytes 2580484
  40.8 25.5 %collective-permute-start.4 = (bf16[1,3,64,1120]{3,2,1,0:T(8,128)(2,1)}, bf16[1,3,64,1120]{3,2,1,0:T(8,128)(2,1)S(1)}, u32[]{:S(2)}, u32[]{:S(2)}) collective-permute-start(bf16[1,3,64,1120]{3,2,1,0:T(8,128)(2,1)} %slice.129), channel_id=1, source_target_pairs={{8,0},{16,8},{24,16},{0,24},{9,1},{17,9},{25,17},{1,25},{10,2},{18... | collective-permute-start | bytes 1290248 | tf_op jit(solution)/shard_map/ppermute | solution.py:33
  42.7 23.7 %copy-start.5 = (bf16[2,3,64,1120]{3,2,1,0:T(8,128)(2,1)}, bf16[2,3,64,1120]{3,2,1,0:T(8,128)(2,1)S(1)}, u32[]{:S(2)}) copy-start(bf16[2,3,64,1120]{3,2,1,0:T(8,128)(2,1)S(1)} %collective-permute-done.2) | copy-start | bytes 2580484
  42.7 23.6 %collective-permute-start.3 = (bf16[1,3,64,1120]{3,2,1,0:T(8,128)(2,1)S(1)}, bf16[1,3,64,1120]{3,2,1,0:T(8,128)(2,1)S(1)}, u32[]{:S(2)}, u32[]{:S(2)}) collective-permute-start(bf16[1,3,64,1120]{3,2,1,0:T(8,128)(2,1)S(1)} %slice.128), channel_id=1, source_target_pairs={{0,8},{8,16},{16,24},{24,0},{1,9},{9,17},{17,25},{25,1},{2,10},{10... | collective-permute-start | bytes 1290248 | tf_op jit(solution)/shard_map/ppermute | solution.py:32
  47.9 39.4 %all-to-all-start = ((bf16[16,112,128]{2,1,0:T(8,128)(2,1)}), bf16[16,112,128]{2,1,0:T(8,128)(2,1)}, u32[]{:S(2)}, u32[]{:S(2)}) async-start(bf16[16,112,128]{2,1,0:T(8,128)(2,1)} %broadcast_in_dim.23), calls=%async_computation | async-start | bytes 917504 | tf_op jit(solution)/shard_map/all_to_all | solution.py:221
  68.5 42.0 %copy-start = (bf16[4,2,3,64,1120]{4,3,2,1,0:T(8,128)(2,1)}, bf16[4,2,3,64,1120]{4,3,2,1,0:T(8,128)(2,1)S(1)}, u32[]{:S(2)}) copy-start(bf16[4,2,3,64,1120]{4,3,2,1,0:T(8,128)(2,1)S(1)} %pad_maximum_fusion.mine_ref) | copy-start | bytes 10321924
  68.5 68.0 %collective-permute-start.5 = (bf16[4,2,3,64,1120]{4,3,2,1,0:T(8,128)(2,1)S(1)}, bf16[4,2,3,64,1120]{4,3,2,1,0:T(8,128)(2,1)}, u32[]{:S(2)}, u32[]{:S(2)}) collective-permute-start(bf16[4,2,3,64,1120]{4,3,2,1,0:T(8,128)(2,1)S(1)} %pad_maximum_fusion.mine_ref), channel_id=1, source_target_pairs={{0,1},{1,0},{2,3},{3,2},{4,5},{5,4},{6,7},{7,6},{8,9},{9,8},{10,11... | collective-permute-start | bytes 10321928 | tf_op jit(solution)/shard_map/ppermute | solution.py:241
  87.3 10.7 %collective-permute-start.8 = (bf16[16,112,128]{2,1,0:T(8,128)(2,1)}, bf16[16,112,128]{2,1,0:T(8,128)(2,1)}, u32[]{:S(2)}, u32[]{:S(2)}) collective-permute-start(bf16[16,112,128]{2,1,0:T(8,128)(2,1)} %all-to-all-done), channel_id=1, source_target_pairs={{0,128},{128,256},{256,384},{384,0},{1,129},{129,257},{257,385},{3... | collective-permute-start | bytes 1376264 | tf_op jit(solution)/shard_map/ppermute | solution.py:30
  91.1 10.8 %collective-permute-start.7 = (bf16[16,112,128]{2,1,0:T(8,128)(2,1)}, bf16[16,112,128]{2,1,0:T(8,128)(2,1)S(1)}, u32[]{:S(2)}, u32[]{:S(2)}) collective-permute-start(bf16[16,112,128]{2,1,0:T(8,128)(2,1)} %all-to-all-done), channel_id=1, source_target_pairs={{128,0},{256,128},{384,256},{0,384},{129,1},{257,129},{385,257},{1... | collective-permute-start | bytes 1376264 | tf_op jit(solution)/shard_map/ppermute | solution.py:31
  99.0 8.5 %collective-permute-start.9 = (bf16[8,112,128]{2,1,0:T(8,128)(2,1)S(1)}, bf16[8,112,128]{2,1,0:T(8,128)(2,1)S(1)}, u32[]{:S(2)}, u32[]{:S(2)}) collective-permute-start(bf16[8,112,128]{2,1,0:T(8,128)(2,1)S(1)} %slice.142), channel_id=1, source_target_pairs={{0,128},{128,256},{256,384},{384,0},{1,129},{129,257},{257,385},{3... | collective-permute-start | bytes 688136 | tf_op jit(solution)/shard_map/ppermute | solution.py:32
  102.0 8.4 %collective-permute-start.10 = (bf16[8,112,128]{2,1,0:T(8,128)(2,1)S(1)}, bf16[8,112,128]{2,1,0:T(8,128)(2,1)S(1)}, u32[]{:S(2)}, u32[]{:S(2)}) collective-permute-start(bf16[8,112,128]{2,1,0:T(8,128)(2,1)S(1)} %slice.143), channel_id=1, source_target_pairs={{128,0},{256,128},{384,256},{0,384},{129,1},{257,129},{385,257},{1... | collective-permute-start | bytes 688136 | tf_op jit(solution)/shard_map/ppermute | solution.py:33
  113.4 1.3 copy-start.1
  119.4 1.6 copy-start.2
  144.5 33.0 %collective-permute-start.11 = (bf16[4,3,2,64,128]{4,3,2,1,0:T(8,128)(2,1)}, bf16[4,3,2,64,128]{4,3,2,1,0:T(8,128)(2,1)S(1)}, u32[]{:S(2)}, u32[]{:S(2)}) collective-permute-start(bf16[4,3,2,64,128]{4,3,2,1,0:T(8,128)(2,1)} %shard_map.78), channel_id=1, source_target_pairs={{0,24},{8,0},{16,8},{24,16},{1,25},{9,1},{17,9},{25,17},{2,26},{10... | collective-permute-start | bytes 1179656 | tf_op jit(solution)/shard_map/ppermute | solution.py:269
  155.9 21.6 %collective-permute-start.12 = (bf16[4,3,2,64,128]{4,3,2,1,0:T(8,128)(2,1)}, bf16[4,3,2,64,128]{4,3,2,1,0:T(8,128)(2,1)S(1)}, u32[]{:S(2)}, u32[]{:S(2)}) collective-permute-start(bf16[4,3,2,64,128]{4,3,2,1,0:T(8,128)(2,1)} %shard_map.79), channel_id=1, source_target_pairs={{0,16},{8,24},{16,0},{24,8},{1,17},{9,25},{17,1},{25,9},{2,18},{10... | collective-permute-start | bytes 1179656 | tf_op jit(solution)/shard_map/ppermute | solution.py:269
  166.6 14.4 %collective-permute-start.13 = (bf16[4,3,2,64,128]{4,3,2,1,0:T(8,128)(2,1)}, bf16[4,3,2,64,128]{4,3,2,1,0:T(8,128)(2,1)S(1)}, u32[]{:S(2)}, u32[]{:S(2)}) collective-permute-start(bf16[4,3,2,64,128]{4,3,2,1,0:T(8,128)(2,1)} %shard_map.80), channel_id=1, source_target_pairs={{0,8},{8,16},{16,24},{24,0},{1,9},{9,17},{17,25},{25,1},{2,10},{10... | collective-permute-start | bytes 1179656 | tf_op jit(solution)/shard_map/ppermute | solution.py:269
  176.5 14.1 %copy-start.3 = (bf16[4,3,2,64,128]{4,3,2,1,0:T(8,128)(2,1)S(1)}, bf16[4,3,2,64,128]{4,3,2,1,0:T(8,128)(2,1)}, u32[]{:S(2)}) copy-start(bf16[4,3,2,64,128]{4,3,2,1,0:T(8,128)(2,1)} %shard_map.77) | copy-start | bytes 1179652
  181.0 10.9 %collective-permute-start.14 = (bf16[4,2,3,2,64,128]{5,4,3,2,1,0:T(8,128)(2,1)S(1)}, bf16[4,2,3,2,64,128]{5,4,3,2,1,0:T(8,128)(2,1)S(1)}, u32[]{:S(2)}, u32[]{:S(2)}) collective-permute-start(bf16[4,2,3,2,64,128]{5,4,3,2,1,0:T(8,128)(2,1)S(1)} %pad_maximum_fusion.5), channel_id=1, source_target_pairs={{0,1},{1,0},{2,3},{3,2},{4,5},{5,4},{6,7},{7,6},{8,9},{9,8},{10,11... | collective-permute-start | bytes 2359304 | tf_op jit(solution)/shard_map/ppermute | solution.py:273
  192.0 0.9 copy-start.6

commit v3 on v2

--- a/solution.py
+++ b/solution.py
@@ -1,3 +1,5 @@
+import functools
+
 import jax
 import jax.numpy as jnp
 from jax import lax
@@ -15,11 +17,12 @@
 REST = HALF - CORE
 TAIL = 2 * REST
 FOLD = DEPTH // 2
-BLOCK = 112
 TABLE = DEPTH + FOLD
 SPAN = 3
 OUT_ROWS = 4
 COLS = 64
+MAIN = 80
+SIDE = 48
 GROUPS = 6
 
 
@@ -34,17 +37,24 @@
     return mine, after, low, high, before
 
 
-def mix_kernel(flag_ref, mine_ref, other_ref, w_ref, table_ref, out_ref, pre_ref, e_ref, m_ref):
-    core = flag_ref[2]
+def sigmoid(v):
+    return 0.5 + 0.5 * jnp.tanh(0.5 * v)
+
+
+def mix_kernel(flag_ref, *refs, slot):
+    parts, (w_ref, table_ref, out_ref, x_ref, pre_ref, e_ref, m_ref) = refs[:4], refs[4:]
+    core, first_in, last_in = flag_ref[0], flag_ref[1 + 2 * slot], flag_ref[2 + 2 * slot]
     n_part = 2 * SPAN * COLS
-    for src, ref in enumerate((mine_ref, other_ref)):
-        x = ref[...].reshape(n_part, ref.shape[-1])
-        for n in range(GROUPS // 2):
-            wide = jnp.dot(
-                x, w_ref[:, 2 * n * LANES : 2 * (n + 1) * LANES], preferred_element_type=jnp.float32
-            )
-            pre_ref[2 * n, pl.ds(src * n_part, n_part), :] = wide[:, :LANES]
-            pre_ref[2 * n + 1, pl.ds(src * n_part, n_part), :] = wide[:, LANES:]
+    for i, ref in enumerate(parts):
+        x_ref[pl.ds(i * SPAN * COLS, SPAN * COLS), :] = ref[...].reshape(SPAN * COLS, -1)
+    for n in range(GROUPS // 2):
+        wide = jnp.dot(
+            x_ref[...],
+            w_ref[:, 2 * n * LANES : 2 * (n + 1) * LANES],
+            preferred_element_type=jnp.float32,
+        )
+        pre_ref[2 * n] = wide[:, :LANES]
+        pre_ref[2 * n + 1] = wide[:, LANES:]
 
     col = lax.broadcasted_iota(jnp.int32, (COLS, LANES), 0)
     lane = lax.broadcasted_iota(jnp.int32, (1, LANES), 1)
@@ -59,10 +69,10 @@
             at = pl.multiple_of(src * n_part + (r - SPAN * late) * COLS, COLS)
             p = pre_ref[g, pl.ds(at, COLS), :] + bias
             t = pre_ref[g, pl.ds(at + SPAN * COLS, COLS), :]
-            sig = jax.nn.sigmoid(p)
+            sig = sigmoid(p)
             pair = (p * sig, sig * (1.0 + p * (1.0 - sig)) * t)
-            last = jnp.where(r == 2 * SPAN - 1, flag_ref[1], 1)
-            inside = jnp.where(r == 0, flag_ref[0], last) > 0
+            last = jnp.where(r == 2 * SPAN - 1, last_in, 1)
+            inside = jnp.where(r == 0, first_in, last) > 0
             for k in range(2):
                 e = jnp.where(inside, pair[k].astype(jnp.bfloat16).astype(jnp.float32), 0.0)
                 e_ref[k, 0, r] = jnp.where(col == 0, 0.0, pltpu.roll(e, 1, 0))
@@ -89,7 +99,7 @@
 
     def gated(q, to, split):
         (vp, gp), (vt, gt) = split(0), split(1)
-        sig = jax.nn.sigmoid(gp)
+        sig = sigmoid(gp)
         gate = gp * sig
         gate_t = sig * (1.0 + gp * (1.0 - sig)) * gt
         out_ref[q, to, 0] = (vp * gate).astype(jnp.bfloat16)
@@ -117,17 +127,22 @@
     lax.fori_loop(0, OUT_ROWS, rows, 0)
 
 
-def mix(flags, mine, others, weights, table, slot):
+def mix(flags, parts, weights, table, slot):
     whole = pl.BlockSpec(memory_space=pltpu.VMEM)
-    part = pl.BlockSpec((1,) + mine.shape[1:], lambda i: (slot, 0, 0, 0, 0))
+    channels = weights.shape[0]
+
+    def part(at):
+        return pl.BlockSpec((1, 1, SPAN, COLS, channels), lambda i: (*at, 0, 0, 0))
+
     n_tok = 4 * SPAN * COLS
     return pl.pallas_call(
-        mix_kernel,
+        functools.partial(mix_kernel, slot=slot),
         grid=(1,),
         out_shape=jax.ShapeDtypeStruct((OUT_ROWS, 3, 2, COLS, LANES), jnp.bfloat16),
-        in_specs=[pl.BlockSpec(memory_space=pltpu.SMEM), part, part, whole, whole],
+        in_specs=[pl.BlockSpec(memory_space=pltpu.SMEM)] + [part(at) for _, at in parts] + [whole, whole],
         out_specs=whole,
         scratch_shapes=[
+            pltpu.VMEM((n_tok, channels), jnp.bfloat16),
             pltpu.VMEM((GROUPS, n_tok, LANES), jnp.float32),
             pltpu.VMEM((2, 3, 2 * SPAN, COLS, LANES), jnp.float32),
             pltpu.VMEM((GROUPS, 2, OUT_ROWS, COLS, LANES), jnp.float32),
@@ -135,7 +150,81 @@
         cost_estimate=pl.CostEstimate(
             flops=2 * n_tok * weights.size, bytes_accessed=5_000_000, transcendentals=1_000_000
         ),
-    )(flags, mine, others, weights, table)
+    )(flags, *[array for array, _ in parts], weights, table)
+
+
+def order_kernel(chosen_ref, own, after, low, high, before, w_ref, table_ref):
+    def block(j, zh, zl):
+        if j == 2:
+            return (low, 4 * zh + zl) if zh < 2 else (high, 4 * (zh - 2) + zl)
+        return {0: own, 1: after, 3: before}[j], 4 * zh + zl
+
+    def part(zl, first, rows):
+        chunks = []
+        for j in range(4):
+            for zh in range(4):
+                ref, at = block(j, zh, zl)
+                chunks.append(ref[at, pl.ds(first, rows), :])
+        return jnp.concatenate(chunks, 0)
+
+    lane = lax.broadcasted_iota(jnp.int32, (1, LANES), 1)
+    n_main, n_side = 16 * MAIN, 16 * SIDE
+    pick = lambda first, count, w: jnp.dot(
+        chosen_ref[:, first : first + count], w, preferred_element_type=jnp.float32
+    )
+    for pair in range(2):
+        zls = (2 * pair, 2 * pair + 1)
+        main = jnp.concatenate([part(zl, 0, MAIN) for zl in zls], 1)
+        side = jnp.concatenate([part(zl, MAIN - 16, SIDE) for zl in zls], 1)
+        w_ref[:, 2 * pair * LANES : 2 * (pair + 1) * LANES] = pick(0, n_main, main).astype(jnp.bfloat16)
+        a, b = pick(n_main, n_side, side), pick(n_main + n_side, n_side, side)
+        even = a[:, :LANES] + pltpu.roll(b[:, :LANES], LANES - TAIL, 1)
+        odd = jnp.where(lane < 2 * TAIL, pltpu.roll(a[:, LANES:], TAIL, 1) + b[:, LANES:], 0.0)
+        w_ref[:, (4 + pair) * LANES : (5 + pair) * LANES] = jnp.where(lane < TAIL, even, odd).astype(
+            jnp.bfloat16
+        )
+    for i in range(11):
+        at, row = 4 * (i // 3), TABLE + i % 3
+        line = lambda zl, r: own[at + zl, pl.ds(r, 1), :].astype(jnp.float32)
+        for zl in range(4):
+            table_ref[zl, pl.ds(i, 1), :] = line(zl, row)
+        for pair in range(2):
+            odd = jnp.where(lane < 2 * TAIL, pltpu.roll(line(2 * pair + 1, row + 3), TAIL, 1), 0.0)
+            table_ref[4 + pair, pl.ds(i, 1), :] = jnp.where(lane < TAIL, line(2 * pair, row + 3), odd)
+
+
+def in_order(chosen, pieces):
+    whole = pl.BlockSpec(memory_space=pltpu.VMEM)
+    channels = chosen.shape[0]
+    return pl.pallas_call(
+        order_kernel,
+        out_shape=(
+            jax.ShapeDtypeStruct((channels, GROUPS * LANES), jnp.bfloat16),
+            jax.ShapeDtypeStruct((GROUPS, 12, LANES), jnp.float32),
+        ),
+        in_specs=[whole] * 6,
+        out_specs=(whole, whole),
+        cost_estimate=pl.CostEstimate(
+            flops=1024 * chosen.size, bytes_accessed=10_000_000, transcendentals=0
+        ),
+    )(chosen, *pieces)
+
+
+def chooser(channels, x):
+    n_main, n_side = 16 * MAIN, 16 * SIDE
+    k = lax.broadcasted_iota(jnp.int32, (1, n_main + 2 * n_side), 1)
+    s = k - n_main
+    second = (s >= n_side).astype(jnp.int32)
+    s = s - n_side * second
+    in_main = k < n_main
+    unit = jnp.where(in_main, k // MAIN, s // SIDE)
+    row = jnp.where(in_main, k % MAIN, s % SIDE - (DEPTH - MAIN + 16))
+    limit = jnp.where(in_main, DEPTH, FOLD)
+    source = ((x + unit // 4) % 4) * 4 * DEPTH + (unit % 4) * DEPTH + row
+    source = source + jnp.where(in_main, 0, FOLD * second)
+    source = jnp.where((row >= 0) & (row < limit), source, -1)
+    channel = lax.broadcasted_iota(jnp.int32, (channels, k.shape[1]), 0)
+    return (channel == source).astype(jnp.bfloat16)
 
 
 def weave_kernel(flag_ref, keep_ref, take_ref, *out):
@@ -237,34 +326,26 @@
         1,
     )
     own, after, low, high, before = ring_pieces(mine, "y")
-    mine = jnp.stack([own, after, jnp.concatenate([low, high], 0), before])
-    others = lax.ppermute(mine, "core", across)
-
-    own, after, low, high, before = ring_pieces(column, "x")
-    turned = jnp.concatenate([own, after, low, high, before], 0).reshape(4, 4, 4, BLOCK, LANES)
-    turned = jnp.concatenate([turned, turned[:3]], 0)
-    ordered = lax.dynamic_slice_in_dim(turned, (4 - x) % 4, 4, 0).reshape(16, 4, BLOCK, LANES)
-    first = ordered[:, :, :DEPTH].transpose(0, 2, 1, 3).reshape(channels, 4 * LANES)
-    folded = ordered[:, :, DEPTH:TABLE]
-    second = jnp.concatenate([folded[..., :TAIL], folded[..., TAIL : 2 * TAIL]], 2)
-    tails = lambda t, n: jnp.pad(
-        t.transpose(0, 2, 1, 3).reshape(n, 2, 2 * TAIL), ((0, 0), (0, 0), (0, LANES - 2 * TAIL))
-    )
-    weights = jnp.concatenate([first, tails(second, channels).reshape(channels, 2 * LANES)], 1)
-    extra = ordered[:4, :, TABLE : TABLE + 6]
-    table = jnp.concatenate(
-        [
-            extra[:, :, :3].transpose(0, 2, 1, 3).reshape(12, 4, LANES),
-            tails(extra[:, :, 3:, :TAIL], 12),
-        ],
-        1,
-    ).transpose(1, 0, 2).astype(jnp.float32)
-
+    near = jnp.stack([own, after, before])
+    low, high = low[None], high[None]
+    near_other = lax.ppermute(near, "core", across)
+    low_other = lax.ppermute(low, "core", across)
+    high_other = lax.ppermute(high, "core", across)
+    parts = {
+        i: [(near, (at, 0)), (near, (at, 1)), (near_other, (at, 0)), (near_other, (at, 1))]
+        for i, at in ((0, 0), (1, 1), (3, 2))
+    }
+    parts[2] = [(a, (0, 0)) for a in (low, high, low_other, high_other)]
+
+    chosen, column = lax.optimization_barrier((chooser(channels, x), column))
+    weights, table = in_order(chosen, ring_pieces(column, "x"))
+
+    chips = 4 * ((y + jnp.arange(4)) % 4) + zl
+    inside = jnp.stack([chips > 0, chips < 15], 1).astype(jnp.int32)
+    flags = jnp.concatenate([core[None], inside.reshape(8)])
     results = {}
-    for turn in (2, 1, 3, 0):
-        chip = 4 * ((y + turn) % 4) + zl
-        flags = jnp.stack([(chip > 0).astype(jnp.int32), (chip < 15).astype(jnp.int32), core])
-        done = mix(flags, mine, others, weights, table, turn)
+    for turn in (1, 2, 3, 0):
+        done = mix(flags, parts[turn], weights, table, turn)
         if turn:
             done = lax.ppermute(done, "y", [(i, (i + turn) % 4) for i in range(4)])
         results[(4 - turn) % 4] = done

time: 198 us -> 176 us (0.89)
  waiting for transfers between devices: 43.6 us -> 16.7 us
  local copies, waits for them, and re-layouts: 26.9 us -> 16.3 us
  starting transfers between devices: 72.5 us -> 82.6 us
  Pallas kernels: 35.9 us -> 44.4 us
  other arithmetic: 16.6 us -> 14.1 us
    ppermute x1 -> x3, starting transfers between devices: 3.07 us -> 17.7 us  [the longest x1 10.6 us: on_device(): low_other = lax.ppermute(low, 'core', across)]
    ppermute x1, waiting for transfers between devices: 13.8 us -> 0.01 us  [on_device(): lax.ppermute(jnp.where(front, high, low), 'y', [(i, (i + 2) % 4) for i in...]
    all_to_all x1, waiting for transfers between devices: 15.7 us -> 5.42 us  [on_device(): column = lax.all_to_all(sent, ('zh', 'zl'), 0, 0)]
    pallas_call x4 -> x5, Pallas kernels: 32 us -> 40.5 us  [the longest x4 32.4 us: mix(): pl.pallas_call(functools.partial(mix_kernel, slot=slot), grid=(1,), out_s...]
    ppermute x3, waiting for transfers between devices: 3.35 us -> 11.3 us  [on_device(): done = lax.ppermute(done, 'y', [(i, (i + turn) % 4) for i in range(4)])]
    reshape x5 -> x0, local copies, waits for them, and re-layouts: 7.41 us -> none  [the longest x3 5.3 us: on_device(): t.transpose(0, 2, 1, 3).reshape(n, 2, 2 * TAIL)]
    ppermute x1, waiting for transfers between devices: 5.29 us -> 0.01 us  [on_device(): lax.ppermute(edge, ('y', 'zl', 'core'), near + [(b, a) for a, b in near])]
    transpose x7 -> x0, local copies, waits for them, and re-layouts: 5.08 us -> none  [the longest x3 3.25 us: on_device(): t.transpose(0, 2, 1, 3).reshape(n, 2, 2 * TAIL)]
  transfers between devices with their start and end apart: 16 -> 18, of which waited for: 7 -> 3; matrix products, arithmetic and copies ran while one was open for 20% -> 15% of each run, Pallas kernels for 12% -> 18%
where the time goes in v3:
time: 176 us; the launch traced here: 175 us
  starting transfers between devices  82.6 us (47%)
  Pallas kernels  44.4 us (25%)
  waiting for transfers between devices  16.7 us (9%)
  local copies, waits for them, and re-layouts  16.3 us (9%)
  other arithmetic  14.1 us (8%)
    pallas_call x4, Pallas kernels, mix(): pl.pallas_call(functools.partial(mix_kernel, slot=slot), grid=(1,), out_s...  32.4 us
    all_to_all x1, starting transfers between devices, on_device(): column = lax.all_to_all(sent, ('zh', 'zl'), 0, 0)  16.6 us
    ppermute x3, waiting for transfers between devices, on_device(): done = lax.ppermute(done, 'y', [(i, (i + turn) % 4) for i in range(4)])  11.3 us
    ppermute x1, starting transfers between devices, on_device(): low_other = lax.ppermute(low, 'core', across)  10.6 us
    ppermute x3, starting transfers between devices, on_device(): done = lax.ppermute(done, 'y', [(i, (i + turn) % 4) for i in range(4)])  8.89 us
    pallas_call x1, Pallas kernels, in_order(): pl.pallas_call(order_kernel, out_shape=(jax.ShapeDtypeStruct((channels, G...  8.07 us
    ppermute x2, starting transfers between devices, ring_pieces(): low = lax.ppermute(before[:cut], axis, up)  6.87 us
    ppermute x2, starting transfers between devices, ring_pieces(): after = lax.ppermute(mine, axis, down)  6.81 us
  transfers between devices with their start and end apart: 18, of which 3 were waited for; matrix products, arithmetic and copies ran while one was open for 15% of the time, Pallas kernels for 18%

profile of v3, /device:TPU:1, one launch (start us, length us, event | category | flops | bytes accessed | tf_op | source)
XLA Modules:
  0.0 175.2 jit_solution(1347650480502000879)
XLA Ops:
  2.0 4.9 %collective-permute-start = (bf16[2,64,1120]{2,1,0:T(8,128)(2,1)S(1)}, bf16[2,64,1120]{2,1,0:T(8,128)(2,1)S(1)}, u32[]{:S(2)}, u32[]{:S(2)}) collective-permute-start(bf16[2,64,1120]{2,1,0:T(8,128)(2,1)S(1)} %broadcast_select_fusion), channel_id=1, source_target_pairs={{1,2},{3,4},{5,6},{7,8},{9,10},{11,12},{13,14},{15,16},{17,18},{19... | collective-permute-start | bytes 860168 | tf_op jit(solution)/shard_map/ppermute | solution.py:318
  8.0 4.8 %collective-permute-start.4 = (bf16[73,88]{1,0:T(8,128)(2,1)}, bf16[73,88]{1,0:T(8,128)(2,1)}, u32[]{:S(2)}, u32[]{:S(2)}) collective-permute-start(bf16[73,88]{1,0:T(8,128)(2,1)} %broadcast_select_fusion.3), channel_id=1, source_target_pairs={{0,16},{8,24},{16,0},{24,8},{1,17},{9,25},{17,1},{25,9},{2,18},{10... | collective-permute-start | bytes 38552 | tf_op jit(solution)/shard_map/ppermute | solution.py:293
  13.1 3.4 %collective-permute-start.1 = (bf16[2,3,64,1120]{3,2,1,0:T(8,128)(2,1)S(1)}, bf16[2,3,64,1120]{3,2,1,0:T(8,128)(2,1)S(1)}, u32[]{:S(2)}, u32[]{:S(2)}) collective-permute-start(bf16[2,3,64,1120]{3,2,1,0:T(8,128)(2,1)S(1)} %get-tuple-element.11), channel_id=1, source_target_pairs={{8,0},{16,8},{24,16},{0,24},{9,1},{17,9},{25,17},{1,25},{10,2},{18... | collective-permute-start | bytes 2580488 | tf_op jit(solution)/shard_map/ppermute | solution.py:34
  16.6 1.9 %collective-permute-start.2 = (bf16[2,3,64,1120]{3,2,1,0:T(8,128)(2,1)S(1)}, bf16[2,3,64,1120]{3,2,1,0:T(8,128)(2,1)S(1)}, u32[]{:S(2)}, u32[]{:S(2)}) collective-permute-start(bf16[2,3,64,1120]{3,2,1,0:T(8,128)(2,1)S(1)} %get-tuple-element.11), channel_id=1, source_target_pairs={{0,8},{8,16},{16,24},{24,0},{1,9},{9,17},{17,25},{25,1},{2,10},{10... | collective-permute-start | bytes 2580488 | tf_op jit(solution)/shard_map/ppermute | solution.py:33
  22.4 4.0 %concatenate.61 = bf16[112,128]{1,0:T(8,128)(2,1)} concatenate(bf16[70,128]{1,0:T(8,128)(2,1)} %fusion.10, bf16[35,128]{1,0:T(8,128)(2,1)} %maximum_maximum_fusion, bf16[3,128]{1,0:T(4,128)(2,1)} %get-tuple-element.33, bf16[3,128]{1,0:T(4,128)(2,1)S(1)} %get-tuple-element.32, bf16[1,128]{1,0:T(2,128)(2,1)} %broadcast_in_dim.43), dimensions={0} | concatenate | bytes 57344 | tf_op jit(solution)/shard_map/concatenate | solution.py:299
  26.4 1.6 broadcast_in_dim.44
  27.9 16.6 %all-to-all-start = ((bf16[16,112,128]{2,1,0:T(8,128)(2,1)}), bf16[16,112,128]{2,1,0:T(8,128)(2,1)}, u32[]{:S(2)}, u32[]{:S(2)}) async-start(bf16[16,112,128]{2,1,0:T(8,128)(2,1)} %broadcast_in_dim.44), calls=%async_computation | async-start | bytes 917504 | tf_op jit(solution)/shard_map/all_to_all | solution.py:310
  45.9 1.8 %pad_maximum_fusion.refs_0_.refs_1_ = bf16[3,2,3,64,1120]{4,3,2,1,0:T(8,128)(2,1)S(1)} fusion(bf16[1,2,3,64,1120]{4,3,2,1,0:T(8,128)(2,1)} %bitcast.39, bf16[1,2,3,64,1120]{4,3,2,1,0:T(8,128)(2,1)} %bitcast.38, bf16[1,2,3,64,1120]{4,3,2,1,0:T(8,128)(2,1)S(1)} %get-tuple-element.10), kind=kLoop, calls=%fused_computation.2 | loop fusion | flops 2580480 | bytes 5160960 | tf_op jit(solution)/shard_map/stack | solution.py:329
  47.7 5.2 %collective-permute-start.3 = (bf16[3,2,3,64,1120]{4,3,2,1,0:T(8,128)(2,1)S(1)}, bf16[3,2,3,64,1120]{4,3,2,1,0:T(8,128)(2,1)}, u32[]{:S(2)}, u32[]{:S(2)}) collective-permute-start(bf16[3,2,3,64,1120]{4,3,2,1,0:T(8,128)(2,1)S(1)} %pad_maximum_fusion.refs_0_.refs_1_), channel_id=1, source_target_pairs={{0,1},{1,0},{2,3},{3,2},{4,5},{5,4},{6,7},{7,6},{8,9},{9,8},{10,11... | collective-permute-start | bytes 7741448 | tf_op jit(solution)/shard_map/ppermute | solution.py:331
  53.0 5.2 %fusion.chosen_ref = bf16[1120,2816]{1,0:T(8,128)(2,1)} fusion(s32[2816]{0:T(1024)S(1)} %fusion.31), kind=kLoop, calls=%fused_computation.1 | loop fusion | flops 6307840 | bytes 6319104 | tf_op jit(solution)/shard_map/convert_element_type | solution.py:227
  58.2 5.4 %all-to-all-done.own = bf16[16,112,128]{2,1,0:T(8,128)(2,1)} async-done(((bf16[16,112,128]{2,1,0:T(8,128)(2,1)}), bf16[16,112,128]{2,1,0:T(8,128)(2,1)}, u32[]{:S(2)}, u32[]{:S(2)}) %all-to-all-start) | async-done | bytes 458784 | tf_op jit(solution)/shard_map/all_to_all | solution.py:310
  63.6 3.1 %collective-permute-start.6 = (bf16[16,112,128]{2,1,0:T(8,128)(2,1)}, bf16[16,112,128]{2,1,0:T(8,128)(2,1)}, u32[]{:S(2)}, u32[]{:S(2)}) collective-permute-start(bf16[16,112,128]{2,1,0:T(8,128)(2,1)} %all-to-all-done.own), channel_id=1, source_target_pairs={{0,128},{128,256},{256,384},{384,0},{1,129},{129,257},{257,385},{3... | collective-permute-start | bytes 1376264 | tf_op jit(solution)/shard_map/ppermute | solution.py:33
  66.7 3.4 %collective-permute-start.5 = (bf16[16,112,128]{2,1,0:T(8,128)(2,1)}, bf16[16,112,128]{2,1,0:T(8,128)(2,1)}, u32[]{:S(2)}, u32[]{:S(2)}) collective-permute-start(bf16[16,112,128]{2,1,0:T(8,128)(2,1)} %all-to-all-done.own), channel_id=1, source_target_pairs={{128,0},{256,128},{384,256},{0,384},{129,1},{257,129},{385,257},{1... | collective-permute-start | bytes 1376264 | tf_op jit(solution)/shard_map/ppermute | solution.py:34
  70.1 1.8 %slice.110 = bf16[1,3,64,1120]{3,2,1,0:T(8,128)(2,1)} slice(bf16[2,3,64,1120]{3,2,1,0:T(8,128)(2,1)} %copy-done.4), slice={[0:1], [0:3], [0:64], [0:1120]} | slice | bytes 860160 | tf_op jit(solution)/shard_map/slice | solution.py:35
  71.9 5.0 %collective-permute-start.10 = (bf16[1,3,64,1120]{3,2,1,0:T(8,128)(2,1)}, bf16[1,3,64,1120]{3,2,1,0:T(8,128)(2,1)}, u32[]{:S(2)}, u32[]{:S(2)}) collective-permute-start(bf16[1,3,64,1120]{3,2,1,0:T(8,128)(2,1)} %slice.110), channel_id=1, source_target_pairs={{0,8},{8,16},{16,24},{24,0},{1,9},{9,17},{17,25},{25,1},{2,10},{10... | collective-permute-start | bytes 1290248 | tf_op jit(solution)/shard_map/ppermute | solution.py:35
  77.7 1.9 %collective-permute-start.11 = (bf16[1,3,64,1120]{3,2,1,0:T(8,128)(2,1)}, bf16[1,3,64,1120]{3,2,1,0:T(8,128)(2,1)}, u32[]{:S(2)}, u32[]{:S(2)}) collective-permute-start(bf16[1,3,64,1120]{3,2,1,0:T(8,128)(2,1)} %slice.111), channel_id=1, source_target_pairs={{8,0},{16,8},{24,16},{0,24},{9,1},{17,9},{25,17},{1,25},{10,2},{18... | collective-permute-start | bytes 1290248 | tf_op jit(solution)/shard_map/ppermute | solution.py:36
  80.6 1.9 %collective-permute-start.7 = (bf16[8,112,128]{2,1,0:T(8,128)(2,1)S(1)}, bf16[8,112,128]{2,1,0:T(8,128)(2,1)S(1)}, u32[]{:S(2)}, u32[]{:S(2)}) collective-permute-start(bf16[8,112,128]{2,1,0:T(8,128)(2,1)S(1)} %slice.108), channel_id=1, source_target_pairs={{0,128},{128,256},{256,384},{384,0},{1,129},{129,257},{257,385},{3... | collective-permute-start | bytes 688136 | tf_op jit(solution)/shard_map/ppermute | solution.py:35
  83.5 4.6 %collective-permute-start.8 = (bf16[8,112,128]{2,1,0:T(8,128)(2,1)S(1)}, bf16[8,112,128]{2,1,0:T(8,128)(2,1)}, u32[]{:S(2)}, u32[]{:S(2)}) collective-permute-start(bf16[8,112,128]{2,1,0:T(8,128)(2,1)S(1)} %slice.109), channel_id=1, source_target_pairs={{128,0},{256,128},{384,256},{0,384},{129,1},{257,129},{385,257},{1... | collective-permute-start | bytes 688136 | tf_op jit(solution)/shard_map/ppermute | solution.py:36
  88.1 10.6 %collective-permute-start.12 = (bf16[1,1,3,64,1120]{4,3,2,1,0:T(8,128)(2,1)}, bf16[1,1,3,64,1120]{4,3,2,1,0:T(8,128)(2,1)}, u32[]{:S(2)}, u32[]{:S(2)}) collective-permute-start(bf16[1,1,3,64,1120]{4,3,2,1,0:T(8,128)(2,1)} %bitcast.14.refs_0_), channel_id=1, source_target_pairs={{0,1},{1,0},{2,3},{3,2},{4,5},{5,4},{6,7},{7,6},{8,9},{9,8},{10,11... | collective-permute-start | bytes 1290248 | tf_op jit(solution)/shard_map/ppermute | solution.py:332
  98.7 1.9 %collective-permute-start.13 = (bf16[1,1,3,64,1120]{4,3,2,1,0:T(8,128)(2,1)}, bf16[1,1,3,64,1120]{4,3,2,1,0:T(8,128)(2,1)}, u32[]{:S(2)}, u32[]{:S(2)}) collective-permute-start(bf16[1,1,3,64,1120]{4,3,2,1,0:T(8,128)(2,1)} %bitcast.15.refs_1_), channel_id=1, source_target_pairs={{0,1},{1,0},{2,3},{3,2},{4,5},{5,4},{6,7},{7,6},{8,9},{9,8},{10,11... | collective-permute-start | bytes 1290248 | tf_op jit(solution)/shard_map/ppermute | solution.py:333
  102.1 8.1 %shard_map.77 = (bf16[1120,768]{1,0:T(8,128)(2,1)}, f32[6,12,128]{2,1,0:T(8,128)}) custom-call(bf16[1120,2816]{1,0:T(8,128)(2,1)} %fusion.chosen_ref, bf16[16,112,128]{2,1,0:T(8,128)(2,1)} %all-to-all-done.own, bf16[16,112,128]{2,1,0:T(8,128)(2,1)} %collective-permute-done.5.after, bf16[8,112,128]{2,1,0:T(8,128)(2,1)} %copy-done.8, ...), custom_call_target="tpu_custom_call" | custom-call | flops 3229614080 | bytes 10000000 | tf_op jit(solution)/shard_map/pallas_call | solution.py:199
  110.2 8.1 %shard_map.80 = bf16[4,3,2,64,128]{4,3,2,1,0:T(8,128)(2,1)} custom-call(s32[9]{0:T(128)} %pad_add_fusion.1.flag_ref, bf16[1,1,3,64,1120]{4,3,2,1,0:T(8,128)(2,1)} %bitcast.14.refs_0_, bf16[1,1,3,64,1120]{4,3,2,1,0:T(8,128)(2,1)} %bitcast.15.refs_1_, bf16[1,1,3,64,1120]{4,3,2,1,0:T(8,128)(2,1)} %collective-permute-done.12.refs_2_, ...), custom_call_target="tpu_custom_call" | custom-call | flops 1321205760 | bytes 5000000 | tf_op jit(solution)/shard_map/pallas_call | solution.py:138
  118.3 3.5 %collective-permute-start.14 = (bf16[4,3,2,64,128]{4,3,2,1,0:T(8,128)(2,1)}, bf16[4,3,2,64,128]{4,3,2,1,0:T(8,128)(2,1)S(1)}, u32[]{:S(2)}, u32[]{:S(2)}) collective-permute-start(bf16[4,3,2,64,128]{4,3,2,1,0:T(8,128)(2,1)} %shard_map.80), channel_id=1, source_target_pairs={{0,16},{8,24},{16,0},{24,8},{1,17},{9,25},{17,1},{25,9},{2,18},{10... | collective-permute-start | bytes 1179656 | tf_op jit(solution)/shard_map/ppermute | solution.py:350
  121.8 10.3 %collective-permute-done.14 = bf16[4,3,2,64,128]{4,3,2,1,0:T(8,128)(2,1)S(1)} collective-permute-done((bf16[4,3,2,64,128]{4,3,2,1,0:T(8,128)(2,1)}, bf16[4,3,2,64,128]{4,3,2,1,0:T(8,128)(2,1)S(1)}, u32[]{:S(2)}, u32[]{:S(2)}) %collective-permute-start.14) | collective-permute-done | bytes 393248 | tf_op jit(solution)/shard_map/ppermute | solution.py:350
  132.1 8.1 %shard_map.79 = bf16[4,3,2,64,128]{4,3,2,1,0:T(8,128)(2,1)} custom-call(s32[9]{0:T(128)} %pad_add_fusion.1.flag_ref, bf16[3,2,3,64,1120]{4,3,2,1,0:T(8,128)(2,1)} %copy-done, bf16[3,2,3,64,1120]{4,3,2,1,0:T(8,128)(2,1)} %copy-done, bf16[3,2,3,64,1120]{4,3,2,1,0:T(8,128)(2,1)} %collective-permute-done.3.refs_2_.refs_3_, ...), custom_call_target="tpu_custom_call" | custom-call | flops 1321205760 | bytes 5000000 | tf_op jit(solution)/shard_map/pallas_call | solution.py:138
  140.2 3.2 %collective-permute-start.9 = (bf16[4,3,2,64,128]{4,3,2,1,0:T(8,128)(2,1)}, bf16[4,3,2,64,128]{4,3,2,1,0:T(8,128)(2,1)S(1)}, u32[]{:S(2)}, u32[]{:S(2)}) collective-permute-start(bf16[4,3,2,64,128]{4,3,2,1,0:T(8,128)(2,1)} %shard_map.79), channel_id=1, source_target_pairs={{0,24},{8,0},{16,8},{24,16},{1,25},{9,1},{17,9},{25,17},{2,26},{10... | collective-permute-start | bytes 1179656 | tf_op jit(solution)/shard_map/ppermute | solution.py:350
  143.5 8.1 %shard_map.81 = bf16[4,3,2,64,128]{4,3,2,1,0:T(8,128)(2,1)} custom-call(s32[9]{0:T(128)} %pad_add_fusion.1.flag_ref, bf16[3,2,3,64,1120]{4,3,2,1,0:T(8,128)(2,1)} %copy-done, bf16[3,2,3,64,1120]{4,3,2,1,0:T(8,128)(2,1)} %copy-done, bf16[3,2,3,64,1120]{4,3,2,1,0:T(8,128)(2,1)} %collective-permute-done.3.refs_2_.refs_3_, ...), custom_call_target="tpu_custom_call" | custom-call | flops 1321205760 | bytes 5000000 | tf_op jit(solution)/shard_map/pallas_call | solution.py:138
  151.6 2.2 %collective-permute-start.15 = (bf16[4,3,2,64,128]{4,3,2,1,0:T(8,128)(2,1)}, bf16[4,3,2,64,128]{4,3,2,1,0:T(8,128)(2,1)S(1)}, u32[]{:S(2)}, u32[]{:S(2)}) collective-permute-start(bf16[4,3,2,64,128]{4,3,2,1,0:T(8,128)(2,1)} %shard_map.81), channel_id=1, source_target_pairs={{0,8},{8,16},{16,24},{24,0},{1,9},{9,17},{17,25},{25,1},{2,10},{10... | collective-permute-start | bytes 1179656 | tf_op jit(solution)/shard_map/ppermute | solution.py:350
  153.8 8.1 %shard_map.78 = bf16[4,3,2,64,128]{4,3,2,1,0:T(8,128)(2,1)} custom-call(s32[9]{0:T(128)} %pad_add_fusion.1.flag_ref, bf16[3,2,3,64,1120]{4,3,2,1,0:T(8,128)(2,1)} %copy-done, bf16[3,2,3,64,1120]{4,3,2,1,0:T(8,128)(2,1)} %copy-done, bf16[3,2,3,64,1120]{4,3,2,1,0:T(8,128)(2,1)} %collective-permute-done.3.refs_2_.refs_3_, ...), custom_call_target="tpu_custom_call" | custom-call | flops 1321205760 | bytes 5000000 | tf_op jit(solution)/shard_map/pallas_call | solution.py:138
  164.0 4.4 %collective-permute-start.16 = (bf16[4,2,3,2,64,128]{5,4,3,2,1,0:T(8,128)(2,1)S(1)}, bf16[4,2,3,2,64,128]{5,4,3,2,1,0:T(8,128)(2,1)S(1)}, u32[]{:S(2)}, u32[]{:S(2)}) collective-permute-start(bf16[4,2,3,2,64,128]{5,4,3,2,1,0:T(8,128)(2,1)S(1)} %pad_maximum_fusion.3), channel_id=1, source_target_pairs={{0,1},{1,0},{2,3},{3,2},{4,5},{5,4},{6,7},{7,6},{8,9},{9,8},{10,11... | collective-permute-start | bytes 2359304 | tf_op jit(solution)/shard_map/ppermute | solution.py:354
  169.0 1.4 pad_maximum_fusion.1.keep_ref
  171.3 3.9 %shard_map.82 = (bf16[1,2,64,2816]{3,2,1,0:T(8,128)(2,1)}, bf16[1,2,64,2816]{3,2,1,0:T(8,128)(2,1)}) custom-call(s32[2]{0:T(128)} %pad_add_fusion.flag_ref, bf16[4,4,3,2,64,128]{5,4,3,2,1,0:T(8,128)(2,1)} %pad_maximum_fusion.1.keep_ref, bf16[4,2,3,2,64,128]{5,4,3,2,1,0:T(8,128)(2,1)} %copy-done.5), custom_call_target="tpu_custom_call" | custom-call | tf_op jit(solution)/shard_map/pallas_call | solution.py:275
  (73 shorter events, 15.6 us)
Async XLA Ops:
  0.6 6.4 %copy-start.9 = (bf16[176]{0:T(256)(128)(2,1)S(1)}, bf16[176]{0:T(256)(128)(2,1)}, u32[]{:S(2)}) copy-start(bf16[176]{0:T(256)(128)(2,1)} %param.9) | copy-start | bytes 1060
  0.6 6.4 %copy-start.10 = (bf16[176]{0:T(256)(128)(2,1)S(1)}, bf16[176]{0:T(256)(128)(2,1)}, u32[]{:S(2)}) copy-start(bf16[176]{0:T(256)(128)(2,1)} %param.11) | copy-start | bytes 1060
  0.7 6.5 %copy-start.7 = (bf16[9,176]{1,0:T(8,128)(2,1)S(1)}, bf16[9,176]{1,0:T(8,128)(2,1)}, u32[]{:S(2)}) copy-start(bf16[9,176]{1,0:T(8,128)(2,1)} %param.10) | copy-start | bytes 9508
  0.7 6.6 %copy-start.6 = (bf16[70,176]{1,0:T(8,128)(2,1)S(1)}, bf16[70,176]{1,0:T(8,128)(2,1)}, u32[]{:S(2)}) copy-start(bf16[70,176]{1,0:T(8,128)(2,1)} %param.8) | copy-start | bytes 73924
  2.0 10.8 %collective-permute-start = (bf16[2,64,1120]{2,1,0:T(8,128)(2,1)S(1)}, bf16[2,64,1120]{2,1,0:T(8,128)(2,1)S(1)}, u32[]{:S(2)}, u32[]{:S(2)}) collective-permute-start(bf16[2,64,1120]{2,1,0:T(8,128)(2,1)S(1)} %broadcast_select_fusion), channel_id=1, source_target_pairs={{1,2},{3,4},{5,6},{7,8},{9,10},{11,12},{13,14},{15,16},{17,18},{19... | collective-permute-start | bytes 860168 | tf_op jit(solution)/shard_map/ppermute | solution.py:318
  8.0 10.7 %collective-permute-start.4 = (bf16[73,88]{1,0:T(8,128)(2,1)}, bf16[73,88]{1,0:T(8,128)(2,1)}, u32[]{:S(2)}, u32[]{:S(2)}) collective-permute-start(bf16[73,88]{1,0:T(8,128)(2,1)} %broadcast_select_fusion.3), channel_id=1, source_target_pairs={{0,16},{8,24},{16,0},{24,8},{1,17},{9,25},{17,1},{25,9},{2,18},{10... | collective-permute-start | bytes 38552 | tf_op jit(solution)/shard_map/ppermute | solution.py:293
  13.1 31.5 %collective-permute-start.1 = (bf16[2,3,64,1120]{3,2,1,0:T(8,128)(2,1)S(1)}, bf16[2,3,64,1120]{3,2,1,0:T(8,128)(2,1)S(1)}, u32[]{:S(2)}, u32[]{:S(2)}) collective-permute-start(bf16[2,3,64,1120]{3,2,1,0:T(8,128)(2,1)S(1)} %get-tuple-element.11), channel_id=1, source_target_pairs={{8,0},{16,8},{24,16},{0,24},{9,1},{17,9},{25,17},{1,25},{10,2},{18... | collective-permute-start | bytes 2580488 | tf_op jit(solution)/shard_map/ppermute | solution.py:34
  16.6 28.0 %collective-permute-start.2 = (bf16[2,3,64,1120]{3,2,1,0:T(8,128)(2,1)S(1)}, bf16[2,3,64,1120]{3,2,1,0:T(8,128)(2,1)S(1)}, u32[]{:S(2)}, u32[]{:S(2)}) collective-permute-start(bf16[2,3,64,1120]{3,2,1,0:T(8,128)(2,1)S(1)} %get-tuple-element.11), channel_id=1, source_target_pairs={{0,8},{8,16},{16,24},{24,0},{1,9},{9,17},{17,25},{25,1},{2,10},{10... | collective-permute-start | bytes 2580488 | tf_op jit(solution)/shard_map/ppermute | solution.py:33
  27.9 35.7 %all-to-all-start = ((bf16[16,112,128]{2,1,0:T(8,128)(2,1)}), bf16[16,112,128]{2,1,0:T(8,128)(2,1)}, u32[]{:S(2)}, u32[]{:S(2)}) async-start(bf16[16,112,128]{2,1,0:T(8,128)(2,1)} %broadcast_in_dim.44), calls=%async_computation | async-start | bytes 917504 | tf_op jit(solution)/shard_map/all_to_all | solution.py:310
  44.6 1.0 copy-start.2
  44.6 1.3 copy-start.4
  47.7 10.5 %copy-start = (bf16[3,2,3,64,1120]{4,3,2,1,0:T(8,128)(2,1)}, bf16[3,2,3,64,1120]{4,3,2,1,0:T(8,128)(2,1)S(1)}, u32[]{:S(2)}) copy-start(bf16[3,2,3,64,1120]{4,3,2,1,0:T(8,128)(2,1)S(1)} %pad_maximum_fusion.refs_0_.refs_1_) | copy-start | bytes 7741444
  47.7 29.2 %copy-start.3 = (bf16[2,3,64,1120]{3,2,1,0:T(8,128)(2,1)S(1)}, bf16[2,3,64,1120]{3,2,1,0:T(8,128)(2,1)}, u32[]{:S(2)}) copy-start(bf16[2,3,64,1120]{3,2,1,0:T(8,128)(2,1)} %copy-done.2) | copy-start | bytes 2580484
  47.7 84.4 %collective-permute-start.3 = (bf16[3,2,3,64,1120]{4,3,2,1,0:T(8,128)(2,1)S(1)}, bf16[3,2,3,64,1120]{4,3,2,1,0:T(8,128)(2,1)}, u32[]{:S(2)}, u32[]{:S(2)}) collective-permute-start(bf16[3,2,3,64,1120]{4,3,2,1,0:T(8,128)(2,1)S(1)} %pad_maximum_fusion.refs_0_.refs_1_), channel_id=1, source_target_pairs={{0,1},{1,0},{2,3},{3,2},{4,5},{5,4},{6,7},{7,6},{8,9},{9,8},{10,11... | collective-permute-start | bytes 7741448 | tf_op jit(solution)/shard_map/ppermute | solution.py:331
  63.6 16.0 %collective-permute-start.6 = (bf16[16,112,128]{2,1,0:T(8,128)(2,1)}, bf16[16,112,128]{2,1,0:T(8,128)(2,1)}, u32[]{:S(2)}, u32[]{:S(2)}) collective-permute-start(bf16[16,112,128]{2,1,0:T(8,128)(2,1)} %all-to-all-done.own), channel_id=1, source_target_pairs={{0,128},{128,256},{256,384},{384,0},{1,129},{129,257},{257,385},{3... | collective-permute-start | bytes 1376264 | tf_op jit(solution)/shard_map/ppermute | solution.py:33
  66.7 15.8 %collective-permute-start.5 = (bf16[16,112,128]{2,1,0:T(8,128)(2,1)}, bf16[16,112,128]{2,1,0:T(8,128)(2,1)}, u32[]{:S(2)}, u32[]{:S(2)}) collective-permute-start(bf16[16,112,128]{2,1,0:T(8,128)(2,1)} %all-to-all-done.own), channel_id=1, source_target_pairs={{128,0},{256,128},{384,256},{0,384},{129,1},{257,129},{385,257},{1... | collective-permute-start | bytes 1376264 | tf_op jit(solution)/shard_map/ppermute | solution.py:34
  71.9 16.2 %collective-permute-start.10 = (bf16[1,3,64,1120]{3,2,1,0:T(8,128)(2,1)}, bf16[1,3,64,1120]{3,2,1,0:T(8,128)(2,1)}, u32[]{:S(2)}, u32[]{:S(2)}) collective-permute-start(bf16[1,3,64,1120]{3,2,1,0:T(8,128)(2,1)} %slice.110), channel_id=1, source_target_pairs={{0,8},{8,16},{16,24},{24,0},{1,9},{9,17},{17,25},{25,1},{2,10},{10... | collective-permute-start | bytes 1290248 | tf_op jit(solution)/shard_map/ppermute | solution.py:35
  77.7 21.0 %collective-permute-start.11 = (bf16[1,3,64,1120]{3,2,1,0:T(8,128)(2,1)}, bf16[1,3,64,1120]{3,2,1,0:T(8,128)(2,1)}, u32[]{:S(2)}, u32[]{:S(2)}) collective-permute-start(bf16[1,3,64,1120]{3,2,1,0:T(8,128)(2,1)} %slice.111), channel_id=1, source_target_pairs={{8,0},{16,8},{24,16},{0,24},{9,1},{17,9},{25,17},{1,25},{10,2},{18... | collective-permute-start | bytes 1290248 | tf_op jit(solution)/shard_map/ppermute | solution.py:36
  80.6 20.9 %collective-permute-start.7 = (bf16[8,112,128]{2,1,0:T(8,128)(2,1)S(1)}, bf16[8,112,128]{2,1,0:T(8,128)(2,1)S(1)}, u32[]{:S(2)}, u32[]{:S(2)}) collective-permute-start(bf16[8,112,128]{2,1,0:T(8,128)(2,1)S(1)} %slice.108), channel_id=1, source_target_pairs={{0,128},{128,256},{256,384},{384,0},{1,129},{129,257},{257,385},{3... | collective-permute-start | bytes 688136 | tf_op jit(solution)/shard_map/ppermute | solution.py:35
  83.5 18.0 %collective-permute-start.8 = (bf16[8,112,128]{2,1,0:T(8,128)(2,1)S(1)}, bf16[8,112,128]{2,1,0:T(8,128)(2,1)}, u32[]{:S(2)}, u32[]{:S(2)}) collective-permute-start(bf16[8,112,128]{2,1,0:T(8,128)(2,1)S(1)} %slice.109), channel_id=1, source_target_pairs={{128,0},{256,128},{384,256},{0,384},{129,1},{257,129},{385,257},{1... | collective-permute-start | bytes 688136 | tf_op jit(solution)/shard_map/ppermute | solution.py:36
  88.1 22.1 %collective-permute-start.12 = (bf16[1,1,3,64,1120]{4,3,2,1,0:T(8,128)(2,1)}, bf16[1,1,3,64,1120]{4,3,2,1,0:T(8,128)(2,1)}, u32[]{:S(2)}, u32[]{:S(2)}) collective-permute-start(bf16[1,1,3,64,1120]{4,3,2,1,0:T(8,128)(2,1)} %bitcast.14.refs_0_), channel_id=1, source_target_pairs={{0,1},{1,0},{2,3},{3,2},{4,5},{5,4},{6,7},{7,6},{8,9},{9,8},{10,11... | collective-permute-start | bytes 1290248 | tf_op jit(solution)/shard_map/ppermute | solution.py:332
  98.7 11.5 %collective-permute-start.13 = (bf16[1,1,3,64,1120]{4,3,2,1,0:T(8,128)(2,1)}, bf16[1,1,3,64,1120]{4,3,2,1,0:T(8,128)(2,1)}, u32[]{:S(2)}, u32[]{:S(2)}) collective-permute-start(bf16[1,1,3,64,1120]{4,3,2,1,0:T(8,128)(2,1)} %bitcast.15.refs_1_), channel_id=1, source_target_pairs={{0,1},{1,0},{2,3},{3,2},{4,5},{5,4},{6,7},{7,6},{8,9},{9,8},{10,11... | collective-permute-start | bytes 1290248 | tf_op jit(solution)/shard_map/ppermute | solution.py:333
  101.4 0.7 copy-start.8
  118.3 13.8 %collective-permute-start.14 = (bf16[4,3,2,64,128]{4,3,2,1,0:T(8,128)(2,1)}, bf16[4,3,2,64,128]{4,3,2,1,0:T(8,128)(2,1)S(1)}, u32[]{:S(2)}, u32[]{:S(2)}) collective-permute-start(bf16[4,3,2,64,128]{4,3,2,1,0:T(8,128)(2,1)} %shard_map.80), channel_id=1, source_target_pairs={{0,16},{8,24},{16,0},{24,8},{1,17},{9,25},{17,1},{25,9},{2,18},{10... | collective-permute-start | bytes 1179656 | tf_op jit(solution)/shard_map/ppermute | solution.py:350
  140.2 22.7 %collective-permute-start.9 = (bf16[4,3,2,64,128]{4,3,2,1,0:T(8,128)(2,1)}, bf16[4,3,2,64,128]{4,3,2,1,0:T(8,128)(2,1)S(1)}, u32[]{:S(2)}, u32[]{:S(2)}) collective-permute-start(bf16[4,3,2,64,128]{4,3,2,1,0:T(8,128)(2,1)} %shard_map.79), channel_id=1, source_target_pairs={{0,24},{8,0},{16,8},{24,16},{1,25},{9,1},{17,9},{25,17},{2,26},{10... | collective-permute-start | bytes 1179656 | tf_op jit(solution)/shard_map/ppermute | solution.py:350
  151.6 12.3 %collective-permute-start.15 = (bf16[4,3,2,64,128]{4,3,2,1,0:T(8,128)(2,1)}, bf16[4,3,2,64,128]{4,3,2,1,0:T(8,128)(2,1)S(1)}, u32[]{:S(2)}, u32[]{:S(2)}) collective-permute-start(bf16[4,3,2,64,128]{4,3,2,1,0:T(8,128)(2,1)} %shard_map.81), channel_id=1, source_target_pairs={{0,8},{8,16},{16,24},{24,0},{1,9},{9,17},{17,25},{25,1},{2,10},{10... | collective-permute-start | bytes 1179656 | tf_op jit(solution)/shard_map/ppermute | solution.py:350
  161.9 7.1 %copy-start.1 = (bf16[4,3,2,64,128]{4,3,2,1,0:T(8,128)(2,1)S(1)}, bf16[4,3,2,64,128]{4,3,2,1,0:T(8,128)(2,1)}, u32[]{:S(2)}) copy-start(bf16[4,3,2,64,128]{4,3,2,1,0:T(8,128)(2,1)} %shard_map.78) | copy-start | bytes 1179652
  164.0 6.4 %collective-permute-start.16 = (bf16[4,2,3,2,64,128]{5,4,3,2,1,0:T(8,128)(2,1)S(1)}, bf16[4,2,3,2,64,128]{5,4,3,2,1,0:T(8,128)(2,1)S(1)}, u32[]{:S(2)}, u32[]{:S(2)}) collective-permute-start(bf16[4,2,3,2,64,128]{5,4,3,2,1,0:T(8,128)(2,1)S(1)} %pad_maximum_fusion.3), channel_id=1, source_target_pairs={{0,1},{1,0},{2,3},{3,2},{4,5},{5,4},{6,7},{7,6},{8,9},{9,8},{10,11... | collective-permute-start | bytes 2359304 | tf_op jit(solution)/shard_map/ppermute | solution.py:354
  170.4 0.9 copy-start.5
